TPU v7x, 128 devices: a whole 4x4x4 slice. The times are simulated.
128 devices in a mesh: term: 8 (over z, y_lo), pencil: 16 (over x, y_hi, core).
Axes of the slice: x: 4, y: 4 (y_hi: 2, y_lo: 2; y = y_hi * 2 + y_lo), z: 4, core: 2. Of those that a mesh axis runs over, the one named last changes fastest.
Arguments:
- present_acoustic: float32 [512, 16, 512], P('pencil'), may hold values from -6 to 6
- prior_acoustic: float32 [512, 16, 512], P('pencil'), may hold values from -6 to 6
- location_factor: float32 [16, 512, 16, 512], P('term', 'pencil'), may hold values from -1 to 1
- spectral_multiplier: float32 [16, 16, 512, 512], P('term', None, 'pencil'), may hold values from -6 to 6
- medium_kinds: int32 [512, 16, 512], P('pencil', 'term'), may hold values from 0 to 2
- organ_properties: float32 [3, 2], replicated, may hold values from 0.05 to 0.3
- thermal_increase: float32 [512, 16, 512], P('pencil', 'term'), may hold values from -6 to 6
Outputs:
- pressure_final: float32 [512, 16, 512], P('pencil', 'term')
- temperature_final: float32 [512, 16, 512], P('pencil', 'term')
Inputs may be any that keep to these rules, and one draw needn't show every extreme that they name: `medium_kinds`: tissue class of each cell: 0 bone, 1 brain, 2 water.
All inputs are finite; a program needn't handle non-finite values.
Results may differ from a plain program's by a relative error of at most 0.0001.
Values sent between devices are 32-bit elements; how exact they have to be, the bound alone decides.
A program may use at most 128 MiB of HBM per device.

v0:
```python
import math

import jax
import jax.numpy as jnp
from jax import lax
from jax.sharding import PartitionSpec as P

WAVE_STEPS = 2
HEAT_STEPS = 2


DIFFUSION = 0.125


def padded_2(block, sides, width):
    for axis, dim in sides:
        count = lax.axis_size(axis)
        forward = [(i, i + 1) for i in range(count - 1)]
        backward = [(target, source) for source, target in forward]
        low = lax.ppermute(
            lax.slice_in_dim(block, block.shape[dim] - width, None, axis=dim), axis, forward
        )
        high = lax.ppermute(lax.slice_in_dim(block, 0, width, axis=dim), axis, backward)
        block = jnp.concatenate([low, block, high], axis=dim)
    return block


def matmul(left, right):
    return jnp.dot(left, right, precision=lax.Precision.HIGHEST, preferred_element_type=jnp.float32)


def contract(form, left, right):
    return jnp.einsum(
        form, left, right, precision=lax.Precision.HIGHEST, preferred_element_type=jnp.float32
    )


def cos_sin(row_freq, column_frequency, length):
    phase_index = row_freq[:, None] * column_frequency[None, :] % length
    phase_angles = phase_index.astype(jnp.float32) * (2.0 * math.pi / length)
    return (jnp.cos(phase_angles), jnp.sin(phase_angles))


def forward_rows(pressure, z_cosine, z_sine, y_cosine, y_sine):
    real_z = contract("rye,ec->ycr", pressure, z_cosine)
    imag_z = -contract("rye,ec->ycr", pressure, z_sine)
    real_part = contract("ky,ycr->kcr", y_cosine, real_z) + contract("ky,ycr->kcr", y_sine, imag_z)
    imag_part = contract("ky,ycr->kcr", y_cosine, imag_z) - contract("ky,ycr->kcr", y_sine, real_z)
    return jnp.stack([real_part, imag_part])


def forward_columns(spectrum, cosine_table, sine_table):
    length_x = spectrum.shape[3]
    flattened = spectrum.reshape(2, -1, length_x)
    real_part = matmul(flattened[0], cosine_table) + matmul(flattened[1], sine_table)
    imag_part = matmul(flattened[1], cosine_table) - matmul(flattened[0], sine_table)
    return jnp.stack([real_part, imag_part]).reshape(spectrum.shape)


def inverse_columns(weighted, cosine_table, sine_table):
    length_x = weighted.shape[4]
    real_in = weighted[:, 0].reshape(-1, length_x)
    imag_in = weighted[:, 1].reshape(-1, length_x)
    real_part = matmul(real_in, cosine_table) - matmul(imag_in, sine_table)
    imag_part = matmul(imag_in, cosine_table) + matmul(real_in, sine_table)
    inner_shape = (weighted.shape[0],) + weighted.shape[2:]
    return jnp.stack([real_part.reshape(inner_shape), imag_part.reshape(inner_shape)], axis=1)


def stencil_sum(padded):
    center = padded[1:-1, 1:-1, :]
    depth_pad = jnp.pad(center, ((0, 0), (0, 0), (1, 1)))
    near_sum = padded[2:, 1:-1, :] + padded[:-2, 1:-1, :]
    near_sum = near_sum + padded[1:-1, 2:, :] + padded[1:-1, :-2, :]
    near_sum = near_sum + depth_pad[:, :, 2:] + depth_pad[:, :, :-2]
    return (center, near_sum)


def heat_update(center, near_sum, perfuse, source):
    return center + DIFFUSION * (near_sum - 6.0 * center) - perfuse * center + source


def on_device(
    present_acoustic,
    prior_acoustic,
    location_factor,
    spectral_multiplier,
    medium_kinds,
    organ_properties,
    thermal_increase,
):
    term_count = lax.axis_size("term")
    pencil_count = lax.axis_size("pencil")
    rows_local = present_acoustic.shape[0]
    length_y = present_acoustic.shape[1]
    length_z = present_acoustic.shape[2]
    length_x = rows_local * pencil_count
    width_brick = length_y // term_count
    brick_start = lax.axis_index("term") * width_brick
    z_index = jnp.arange(length_z, dtype=jnp.int32)
    x_index = jnp.arange(length_x, dtype=jnp.int32)
    y_index = jnp.arange(length_y, dtype=jnp.int32)
    x_cos, x_sin = cos_sin(x_index, x_index, length_x)
    z_cos, z_sin = cos_sin(z_index, z_index, length_z)
    y_cos, y_sin = cos_sin(y_index, y_index, length_y)
    inverse_norm = 1.0 / (length_x * length_y * length_z)

    def to_brick(values):
        return lax.dynamic_slice_in_dim(values, brick_start, width_brick, 1)

    pick_cos, pick_sin = (z_cos, z_sin)
    previous = prior_acoustic
    current = present_acoustic
    dose_sum = jnp.zeros(medium_kinds.shape, jnp.float32)
    final_brick = dose_sum
    for turn_index in range(WAVE_STEPS):
        rows_spec = forward_rows(current, pick_cos, pick_sin, y_cos, y_sin)
        spectrum = lax.all_to_all(rows_spec, "pencil", split_axis=2, concat_axis=3, tiled=True)
        spectrum = forward_columns(spectrum, x_cos, x_sin)
        weighted = spectral_multiplier[:, None] * spectrum[None]
        term_restored = inverse_columns(weighted, x_cos, x_sin)
        restored = lax.all_to_all(term_restored, "pencil", split_axis=4, concat_axis=3, tiled=True)
        real_in = restored[:, 0]
        imag_in = restored[:, 1]
        real_y = contract("yk,nkzr->nyzr", y_cos, real_in) - contract(
            "yk,nkzr->nyzr", y_sin, imag_in
        )
        imag_y = contract("yk,nkzr->nyzr", y_cos, imag_in) + contract(
            "yk,nkzr->nyzr", y_sin, real_in
        )
        real_part = contract("nyzr,zw->nryw", real_y, z_cos) - contract(
            "nyzr,zw->nryw", imag_y, z_sin
        )
        fields = real_part * inverse_norm
        partial_value = jnp.sum(location_factor * fields, axis=0)
        if turn_index + 1 < WAVE_STEPS:
            summed = lax.psum(partial_value, "term")
            advanced = 2.0 * summed - previous
            advanced_brick = to_brick(advanced)
            dose_sum = advanced_brick * advanced_brick
            previous = current
            current = advanced
        else:
            summed = lax.psum(partial_value, "term")
            final_brick = to_brick(2.0 * summed - previous)
            dose_sum = dose_sum + final_brick * final_brick
    absorb = jnp.where(
        medium_kinds == 0,
        organ_properties[0, 0],
        jnp.where(medium_kinds == 1, organ_properties[1, 0], organ_properties[2, 0]),
    )
    perfuse = jnp.where(
        medium_kinds == 0,
        organ_properties[0, 1],
        jnp.where(medium_kinds == 1, organ_properties[1, 1], organ_properties[2, 1]),
    )
    source = absorb * dose_sum
    present_thermal = thermal_increase
    for turn_index in range(HEAT_STEPS):
        padded = padded_2(present_thermal, (("term", 1), ("pencil", 0)), 1)
        center, near_sum = stencil_sum(padded)
        present_thermal = heat_update(center, near_sum, perfuse, source)
    return (final_brick, present_thermal)


def solution(mesh):
    return jax.shard_map(
        on_device,
        mesh=mesh,
        in_specs=(
            P("pencil", None, None),
            P("pencil", None, None),
            P("term", "pencil", None, None),
            P("term", None, "pencil", None),
            P("pencil", "term", None),
            P(),
            P("pencil", "term", None),
        ),
        out_specs=(P("pencil", "term", None), P("pencil", "term", None)),
        check_vma=False,
    )
```

profile of v0, /device:TPU:33, one launch (start us, length us, event | category | flops | bytes accessed | tf_op | source)
XLA Modules:
  0.0 922.0 jit_solution(16098968295826274039)
XLA Ops:
  7.2 8.2 fusion.27
  15.4 7.2 convolution_bitcast_fusion.1
  28.9 7.6 copy.171
  36.6 7.4 reshape.35
  44.0 35.8 %all_to_all.66 = f32[16,1,32768]{2,1,0:T(1,128)} all-to-all(f32[16,1,32768]{2,1,0:T(1,128)S(1)} %reshape.35), channel_id=1, replica_groups=mesh['term'=8,'pencil'=16] {'pencil'}, dimensions={0} | all-to-all | bytes 4194304 | tf_op jit(solution)/shard_map/all_to_all | solution.py:118
  80.3 7.3 reduce
  92.8 8.2 copy.267
  140.5 8.6 fusion.69
  149.1 8.5 fusion.67
  157.7 8.8 convolution_subtract_fusion.1
  166.5 7.6 copy.173
  174.1 10.3 %convolution_add_fusion.1 = f32[1024,512]{1,0:T(8,128)S(1)} fusion(f32[1024,512]{1,0:T(8,128)} %fusion.67, f32[1024,512]{1,0:T(8,128)} %bitcast.215), kind=kOutput, calls=%fused_computation.40 | convolution fusion | flops 3225419776 | bytes 6291456 | tf_op jit(solution)/shard_map/dot_general | solution.py:29
  184.4 7.6 copy.174
  192.0 11.8 %fusion.319 = f32[512,2,2,16,32]{4,3,2,1,0:T(8,128)} fusion(f32[2,1,16,32,512]{3,2,1,0,4:T(8,128)} %copy.174, f32[2,1,16,32,512]{3,2,1,0,4:T(8,128)} %copy.173), kind=kLoop, calls=%fused_computation.346 | loop fusion | flops 1048576 | bytes 8388608
  203.8 16.0 %reshape.37 = f32[16,1,65536]{2,1,0:T(1,128)} reshape(f32[512,2,2,16,32]{4,3,2,1,0:T(8,128)} %fusion.319) | data formatting | bytes 8388608
  219.8 56.3 %all_to_all.67 = f32[16,1,65536]{2,1,0:T(1,128)} all-to-all(f32[16,1,65536]{2,1,0:T(1,128)} %reshape.37), channel_id=1, replica_groups=mesh['term'=8,'pencil'=16] {'pencil'}, dimensions={0} | all-to-all | bytes 8388608 | tf_op jit(solution)/shard_map/all_to_all | solution.py:122
  276.1 13.7 %reduce.1 = f32[16,65536]{1,0:T(8,128)} reduce(f32[16,1,65536]{2,1,0:T(1,128)} %all_to_all.67, f32[]{:T(128)} %broadcast.208), dimensions={1}, to_apply=%all_to_all.51.reduce_sub_computation | reduce | bytes 8388612 | tf_op jit(solution)/shard_map/all_to_all | solution.py:122
  289.8 15.1 %reshape.38 = f32[512,2,2,16,32]{4,3,2,1,0:T(8,128)} reshape(f32[16,65536]{1,0:T(8,128)} %reduce.1) | data formatting | bytes 8388608
  304.9 17.8 %copy.220 = f32[2,2,16,16,32,32]{4,3,2,5,0,1:T(8,128)} copy(f32[2,2,16,16,32,32]{4,2,1,0,5,3:T(8,128)} %bitcast.202) | data formatting | bytes 8388608 | tf_op jit(solution)/shard_map/all_to_all | solution.py:122
  322.7 13.1 %reshape.33 = f32[2,2,16,512,32]{3,2,4,0,1:T(8,128)} reshape(f32[2,2,16,16,32,32]{4,3,2,5,0,1:T(8,128)} %copy.220) | data formatting | bytes 8388608 | tf_op jit(solution)/shard_map/all_to_all | solution.py:122
  346.3 8.4 fusion.6
  354.8 11.1 %fusion.1 = f32[32,16,512]{2,0,1:T(8,128)} fusion(f32[512,2,16,32]{0,3,2,1:T(8,128)S(1)} %fusion.6, f32[2,32,16,512]{3,2,1,0:T(8,128)S(1)} %copy-done.11, f32[2,16,512,32]{2,1,3,0:T(8,128)S(1)} %subtract_bitcast_fusion.1), kind=kOutput, calls=%fused_computation.15 | convolution fusion | flops 3226730496 | bytes 7340032 | tf_op jit(solution)/shard_map/nyzr,zw->nryw/dot_general | solution.py:33
  365.9 72.6 %all-reduce.5.cloned.1.call-done = f32[32,16,512]{2,0,1:T(8,128)} async-done(((f32[32,16,512]{2,0,1:T(8,128)}), f32[32,16,512]{2,0,1:T(8,128)}) %all-reduce.5.cloned.1.call-update) | async-done | bytes 1048592 | tf_op jit(solution)/shard_map/psum | solution.py:137
  440.4 6.5 convolution_bitcast_fusion
  459.7 7.6 copy.187
  467.4 7.4 reshape.39
  474.8 40.0 %all_to_all.68 = f32[16,1,32768]{2,1,0:T(1,128)} all-to-all(f32[16,1,32768]{2,1,0:T(1,128)S(1)} %reshape.39), channel_id=1, replica_groups=mesh['term'=8,'pencil'=16] {'pencil'}, dimensions={0} | all-to-all | bytes 4194304 | tf_op jit(solution)/shard_map/all_to_all | solution.py:118
  514.8 7.3 reduce.2
  527.3 8.2 copy.266
  542.9 6.7 fusion.62
  575.4 8.6 fusion.58
  584.0 8.5 fusion.64
  592.6 8.8 convolution_subtract_fusion
  601.4 7.6 copy.189
  609.0 10.3 %convolution_add_fusion = f32[1024,512]{1,0:T(8,128)S(1)} fusion(f32[1024,512]{1,0:T(8,128)} %fusion.64, f32[1024,512]{1,0:T(8,128)} %bitcast.217), kind=kOutput, calls=%fused_computation.38 | convolution fusion | flops 3225419776 | bytes 6291456 | tf_op jit(solution)/shard_map/dot_general | solution.py:29
  619.3 7.6 copy.190
  626.9 11.8 %fusion.318 = f32[512,2,2,16,32]{4,3,2,1,0:T(8,128)} fusion(f32[2,1,16,32,512]{3,2,1,0,4:T(8,128)} %copy.190, f32[2,1,16,32,512]{3,2,1,0,4:T(8,128)} %copy.189), kind=kLoop, calls=%fused_computation.345 | loop fusion | flops 1048576 | bytes 8388608
  638.7 16.0 %reshape.41 = f32[16,1,65536]{2,1,0:T(1,128)} reshape(f32[512,2,2,16,32]{4,3,2,1,0:T(8,128)} %fusion.318) | data formatting | bytes 8388608
  660.7 52.4 %all-to-all-done.3 = f32[16,1,65536]{2,1,0:T(1,128)} async-done(((f32[16,1,65536]{2,1,0:T(1,128)}), f32[16,1,65536]{2,1,0:T(1,128)}, u32[]{:S(2)}, u32[]{:S(2)}) %all-to-all-start.3) | async-done | bytes 4194336 | tf_op jit(solution)/shard_map/all_to_all | solution.py:122
  713.1 13.7 %reduce.3 = f32[16,65536]{1,0:T(8,128)} reduce(f32[16,1,65536]{2,1,0:T(1,128)} %all-to-all-done.3, f32[]{:T(128)} %broadcast.208), dimensions={1}, to_apply=%all_to_all.58.reduce_sub_computation | reduce | bytes 8388612 | tf_op jit(solution)/shard_map/all_to_all | solution.py:122
  726.8 15.1 %reshape.42 = f32[512,2,2,16,32]{4,3,2,1,0:T(8,128)} reshape(f32[16,65536]{1,0:T(8,128)} %reduce.3) | data formatting | bytes 8388608
  741.9 17.8 %copy.222 = f32[2,2,16,16,32,32]{4,3,2,5,0,1:T(8,128)} copy(f32[2,2,16,16,32,32]{4,2,1,0,5,3:T(8,128)} %bitcast.203) | data formatting | bytes 8388608 | tf_op jit(solution)/shard_map/all_to_all | solution.py:122
  759.7 13.1 %reshape.34 = f32[2,2,16,512,32]{3,2,4,0,1:T(8,128)} reshape(f32[2,2,16,16,32,32]{4,3,2,5,0,1:T(8,128)} %copy.222) | data formatting | bytes 8388608 | tf_op jit(solution)/shard_map/all_to_all | solution.py:122
  783.3 8.3 fusion.2
  791.6 11.1 %fusion = f32[32,16,512]{2,0,1:T(8,128)} fusion(f32[512,2,16,32]{0,3,2,1:T(8,128)S(1)} %fusion.2, f32[2,32,16,512]{3,2,1,0:T(8,128)S(1)} %copy-done.12, f32[2,16,512,32]{2,1,3,0:T(8,128)S(1)} %subtract_bitcast_fusion), kind=kOutput, calls=%fused_computation.13 | convolution fusion | flops 3226730496 | bytes 7340032 | tf_op jit(solution)/shard_map/nyzr,zw->nryw/dot_general | solution.py:33
  813.4 9.8 %collective-permute-start.3 = (f32[1,4,512]{2,0,1:T(1,128)S(1)}, f32[1,4,512]{2,0,1:T(1,128)S(1)}, u32[]{:S(2)}, u32[]{:S(2)}) collective-permute-start(f32[1,4,512]{2,0,1:T(1,128)S(1)} %get-tuple-element.23), channel_id=1, source_target_pairs={{0,1},{1,2},{2,3},{3,4},{4,5},{5,6},{6,7},{7,8},{8,9},{9,10},{10,1... | collective-permute-start | bytes 24584 | tf_op jit(solution)/shard_map/ppermute | solution.py:20
  825.7 58.5 %all-reduce.7.cloned.1.call-done = f32[32,16,512]{2,0,1:T(8,128)} async-done(((f32[32,16,512]{2,0,1:T(8,128)}), f32[32,16,512]{2,0,1:T(8,128)}) %all-reduce.7.cloned.1.call-update) | async-done | bytes 1048592 | tf_op jit(solution)/shard_map/psum | solution.py:144
  896.6 8.4 collective-permute-start.6
  (103 shorter events, 166.3 us)
Async XLA Ops:
  7.2 8.3 copy-start.7
  7.2 431.3 %all-reduce.5.cloned.1.call-start = ((), (), s32[]{:S(2)}) async-start(), calls=%async_computation.4 | async-start | bytes 2097152 | tf_op jit(solution)/shard_map/psum | solution.py:137
  137.5 1.6 copy-start.4
  140.5 8.6 copy-start.2
  335.8 3.9 copy-start
  346.3 8.4 copy-start.11
  354.8 83.7 %copy-start.6 = (f32[32,16,512]{2,1,0:T(8,128)S(1)}, f32[32,16,512]{2,1,0:T(8,128)}, u32[]{:S(2)}) copy-start(f32[32,16,512]{2,1,0:T(8,128)} %param.8) | copy-start | bytes 3145732
  553.2 6.5 copy-start.13
  572.3 1.6 copy-start.5
  575.4 8.6 copy-start.3
  654.7 6.0 copy-start.8
  654.7 58.4 %all-to-all-start.3 = ((f32[16,1,65536]{2,1,0:T(1,128)}), f32[16,1,65536]{2,1,0:T(1,128)}, u32[]{:S(2)}, u32[]{:S(2)}) async-start(f32[16,1,65536]{2,1,0:T(1,128)} %reshape.41), calls=%async_computation.3 | async-start | bytes 8388608 | tf_op jit(solution)/shard_map/all_to_all | solution.py:122
  660.6 223.6 %all-reduce.7.cloned.1.call-start = ((), (), s32[]{:S(2)}) async-start(), calls=%async_computation.5 | async-start | bytes 2097152 | tf_op jit(solution)/shard_map/psum | solution.py:144
  772.8 3.9 copy-start.1
  783.3 8.3 copy-start.12
  791.6 31.6 %copy-start.10 = (f32[3,2]{0,1:T(2,128)S(1)}, f32[3,2]{0,1:T(2,128)}, u32[]{:S(2)}) copy-start(f32[3,2]{0,1:T(2,128)} %param.12) | copy-start | bytes 76
  802.8 81.5 %copy-start.9 = (s32[32,2,512]{2,1,0:T(2,128)S(1)}, s32[32,2,512]{2,1,0:T(2,128)}, u32[]{:S(2)}) copy-start(s32[32,2,512]{2,1,0:T(2,128)} %param.11) | copy-start | bytes 393220
  802.8 6.9 collective-permute-start
  804.9 6.0 collective-permute-start.1
  810.8 14.9 %collective-permute-start.2 = (f32[1,4,512]{2,0,1:T(1,128)S(1)}, f32[1,4,512]{2,0,1:T(1,128)S(1)}, u32[]{:S(2)}, u32[]{:S(2)}) collective-permute-start(f32[1,4,512]{2,0,1:T(1,128)S(1)} %get-tuple-element.22), channel_id=1, source_target_pairs={{1,0},{2,1},{3,2},{4,3},{5,4},{6,5},{7,6},{8,7},{9,8},{10,9},{11,1... | collective-permute-start | bytes 24584 | tf_op jit(solution)/shard_map/ppermute | solution.py:23
  813.4 12.4 %collective-permute-start.3 = (f32[1,4,512]{2,0,1:T(1,128)S(1)}, f32[1,4,512]{2,0,1:T(1,128)S(1)}, u32[]{:S(2)}, u32[]{:S(2)}) collective-permute-start(f32[1,4,512]{2,0,1:T(1,128)S(1)} %get-tuple-element.23), channel_id=1, source_target_pairs={{0,1},{1,2},{2,3},{3,4},{4,5},{5,6},{6,7},{7,8},{8,9},{9,10},{10,1... | collective-permute-start | bytes 24584 | tf_op jit(solution)/shard_map/ppermute | solution.py:20
  889.1 6.2 collective-permute-start.4
  891.4 5.1 collective-permute-start.5
  896.6 13.4 %collective-permute-start.6 = (f32[1,4,512]{2,0,1:T(1,128)S(1)}, f32[1,4,512]{2,0,1:T(1,128)S(1)}, u32[]{:S(2)}, u32[]{:S(2)}) collective-permute-start(f32[1,4,512]{2,0,1:T(1,128)S(1)} %get-tuple-element.20), channel_id=1, source_target_pairs={{1,0},{2,1},{3,2},{4,3},{5,4},{6,5},{7,6},{8,7},{9,8},{10,9},{11,1... | collective-permute-start | bytes 24584 | tf_op jit(solution)/shard_map/ppermute | solution.py:23
  905.0 5.0 collective-permute-start.7
Sparse Core Ops, SparseCore 0:
  366.1 72.3 all-reduce.4
  802.9 81.2 all-reduce.6
where the time goes:
time: 934 us; the launch traced here: 922 us
  local copies, waits for them, and re-layouts  242 us (26%)
  matrix products  224 us (24%)
  waiting for transfers between devices  186 us (20%)
  blocking collectives  132 us (14%)
  other arithmetic  78.9 us (8%)
  starting transfers between devices  43.5 us (5%)
  between operations  15.3 us (2%)
    psum x2, waiting for transfers between devices, on_device(): summed = lax.psum(partial_value, 'term')  131 us
    dot_general x16, matrix products, matmul(): jnp.dot(left, right, precision=lax.Precision.HIGHEST, preferred_element_t...  124 us
    dot_general x24, matrix products, contract(): jnp.einsum(form, left, right, precision=lax.Precision.HIGHEST, preferred_...  100 us
    unnamed x42, local copies, waits for them, and re-layouts  93.7 us
    all_to_all x2, blocking collectives, on_device(): lax.all_to_all(rows_spec, 'pencil', split_axis=2, concat_axis=3, tiled=True)  75.8 us
    all_to_all x4, local copies, waits for them, and re-layouts, on_device(): lax.all_to_all(term_restored, 'pencil', split_axis=4, concat_axis=3, tile...  61.7 us
    all_to_all x1, blocking collectives, on_device(): lax.all_to_all(term_restored, 'pencil', split_axis=4, concat_axis=3, tile...  56.3 us
    all_to_all x1, waiting for transfers between devices, on_device(): lax.all_to_all(term_restored, 'pencil', split_axis=4, concat_axis=3, tile...  52.4 us
  transfers between devices with their start and end apart: 11, of which 6 were waited for; matrix products, arithmetic and copies ran while one was open for 0% of the time, Pallas kernels for 0%

commit v1 on v0

v1 whole, which is shorter than its diff:
```python
import math

import numpy as np

import jax
import jax.numpy as jnp
from jax import lax
from jax.experimental import pallas as pl
from jax.experimental.pallas import tpu as pltpu
from jax.sharding import PartitionSpec as P

WAVE_STEPS = 2
HEAT_STEPS = 2
DIFFUSION = 0.125
MESH = pl.DeviceIdType.MESH
F32 = jnp.float32
BF16 = jnp.bfloat16

NX = 512
NY = 16
NZ = 512
NT = 8
NP = 16
XR = NX // NP
SCALE = 2.0 / (NX * NY * NZ)


def high_low(table):
    high = table.astype(BF16)
    low = (table - high.astype(np.float32)).astype(BF16)
    return np.stack([high, low])


def z_table():
    rows = np.zeros((2, NP, 2, 8, NZ), np.float64)
    z = np.arange(NZ)
    for h in range(2):
        for p in range(NP):
            for i in range(8):
                s = 8 * h + i
                if s == 0 and p == 8:
                    rows[h, p, 0, i] = 1.0
                    rows[h, p, 1, i] = 1.0 - 2.0 * (z % 2)
                    continue
                kz = 32 * p + s
                if s == 0 and p < 8:
                    kz = 32 * p + 16
                angle = 2.0 * math.pi * ((kz * z) % NZ) / NZ
                rows[h, p, 0, i] = np.cos(angle)
                rows[h, p, 1, i] = -np.sin(angle)
    return high_low(rows.reshape(NZ, NZ).astype(np.float32))


def x_table():
    k = np.arange(256)[:, None]
    tables = []
    for c in range(2):
        x = 2 * np.arange(256)[None, :] + c
        angle = 2.0 * math.pi * ((k * x) % NX) / NX
        co, si = np.cos(angle), np.sin(angle)
        tables.append(high_low(np.block([[co, si], [-si, co]]).astype(np.float32)))
    return np.stack(tables)


def split(x):
    high = x.astype(BF16)
    low = (x - high.astype(F32)).astype(BF16)
    return high, low


def dot(a, b, ca, cb):
    return lax.dot_general(a, b, (((ca,), (cb,)), ((), ())), preferred_element_type=F32)


def dot3(a, b, ca, cb):
    return dot(a[0], b[0], ca, cb) + dot(a[0], b[1], ca, cb) + dot(a[1], b[0], ca, cb)


def fft16(re, im, sign):
    n = len(re)
    if n == 1:
        return re, im
    er, ei = fft16(re[0::2], im[0::2], sign)
    orr, oi = fft16(re[1::2], im[1::2], sign)
    half = n // 2
    out_r, out_i = [None] * n, [None] * n
    for k in range(half):
        angle = sign * 2.0 * math.pi * k / n
        c, s = math.cos(angle), math.sin(angle)
        a, b = orr[k], oi[k]
        if k == 0:
            tr, ti = a, b
        elif 4 * k == n:
            tr, ti = (b, -a) if sign < 0 else (-b, a)
        elif abs(abs(c) - abs(s)) < 1e-12:
            r = math.sqrt(0.5)
            sc, ss = math.copysign(1.0, c), math.copysign(1.0, s)
            tr = r * ((a if sc > 0 else -a) - (b if ss > 0 else -b))
            ti = r * ((b if sc > 0 else -b) + (a if ss > 0 else -a))
        else:
            tr = c * a - s * b
            ti = c * b + s * a
        out_r[k], out_i[k] = er[k] + tr, ei[k] + ti
        out_r[k + half], out_i[k + half] = er[k] - tr, ei[k] - ti
    return out_r, out_i


def exchange_groups(tiles):
    rows = tiles[0].shape[0]
    lane = lax.broadcasted_iota(jnp.int32, (rows, 128), 1)
    tiles = list(tiles)
    for bit in (4, 2, 1):
        width = bit * 16
        keep_low = (lane % (2 * width)) < width
        new = list(tiles)
        for i in range(8):
            if i & bit:
                continue
            a, b = tiles[i], tiles[i + bit]
            new[i] = jnp.where(keep_low, a, pltpu.roll(b, width, 1))
            new[i + bit] = jnp.where(keep_low, pltpu.roll(a, 128 - width, 1), b)
        tiles = new
    return tiles


def reverse_lanes(tiles):
    lane = lax.broadcasted_iota(jnp.int32, (8, 128), 1)
    index = (128 - lane) % 128
    moved = [jnp.take_along_axis(x, index, axis=1) for x in tiles]
    return [jnp.where(lane == 0, moved[(4 - a) % 4], moved[3 - a]) for a in range(4)]


def wave_kernel(
    pres, prior, loc, spec, ztab, xtab, final_o, dose_o,
    pres_v, prior_v, loc_v, lr, spec_v, srecv, row0, row0r, amp, bmp, zt, xt,
    cur, prev, dose, fsend, frecv, vsend, agb, w, xo, snd, rcv, psend, rsr,
    lsem, ssem, sx, fs, fr, gs, gr, as0, ar0, as1, ar1, rs, rr,
):
    t = lax.axis_index("term")
    p = lax.axis_index("pencil")

    barrier = pltpu.get_barrier_semaphore()

    @pl.loop(1, NP)
    def _(o):
        pl.semaphore_signal(barrier, inc=1, device_id=(t, lax.rem(p + o, NP)), device_id_type=MESH)

    @pl.loop(1, NT)
    def _(o):
        pl.semaphore_signal(barrier, inc=1, device_id=(lax.rem(t + o, NT), p), device_id_type=MESH)

    loads = [
        pltpu.make_async_copy(src, dst, lsem.at[i])
        for i, (src, dst) in enumerate(
            [(pres, pres_v), (ztab, zt), (xtab, xt), (spec, spec_v), (prior, prior_v), (loc, loc_v)]
        )
    ]
    for load in loads:
        load.start()

    pl.semaphore_wait(barrier, NP + NT - 2)

    def remote(src, dst, send, recv, device):
        return pltpu.make_async_remote_copy(
            src_ref=src, dst_ref=dst, send_sem=send, recv_sem=recv, device_id=device, device_id_type=MESH
        )

    mirror = (t, NP - 1 - p)
    swap = remote(spec.at[:, :, pl.ds(16, 16), :], srecv, sx.at[0], sx.at[1], mirror)
    swap.start()

    loads[0].wait()
    for y in range(2):
        for x in range(XR):
            row = y * XR + (x % 2) * 16 + x // 2
            cur[pl.ds(row, 1), :] = pres_v[x, pl.ds(2 * t + y, 1), :]
    loads[3].wait()
    for q in range(2):
        row0[pl.ds(16 * q, 16), 0, :] = spec_v[q, :, 0, :]
    give = jnp.where(p == 0, 8, lax.rem(NP - p, NP))
    rowcopy = remote(row0, row0r, sx.at[2], sx.at[3], (t, give))

    @pl.when(p < 8)
    def _():
        rowcopy.start()

    loads[4].wait()
    for y in range(2):
        for x in range(XR):
            row = y * XR + (x % 2) * 16 + x // 2
            prev[pl.ds(row, 1), :] = prior_v[x, pl.ds(2 * t + y, 1), :]
    dose[...] = jnp.zeros_like(dose)
    loads[1].wait()
    loads[2].wait()

    lane = lax.broadcasted_iota(jnp.int32, (8, 128), 1)
    sub = lax.broadcasted_iota(jnp.int32, (8, 128), 0)
    flip = (8 - sub) % 8

    def build_amp():
        swap.wait()

        @pl.when(p < 8)
        def _():
            rowcopy.wait_send()

        @pl.when(p >= 8)
        def _():
            rowcopy.wait_recv()

        low_p = jnp.where(p < 8, 1, 0)

        @pl.loop(0, 32)
        def _(n):
            q = n // 16
            ky = lax.rem(n, 16)
            kr = lax.rem(16 - ky, 16)
            pick_own = (sub == 0) & (low_p == 1)
            pick_row = (sub == 0) & (low_p == 0)
            mirrored = [[], []]
            for a in range(4):
                cols = pl.ds(128 * a, 128)
                r0 = srecv[q, kr, pl.ds(0, 8), cols]
                r1 = srecv[q, kr, pl.ds(8, 8), cols]
                extra = jnp.broadcast_to(row0r[16 * q + kr, :, cols], (8, 128))
                f0 = jnp.take_along_axis(r0, flip, axis=0)
                f1 = jnp.take_along_axis(r1, flip, axis=0)
                m0 = jnp.where(sub == 0, r0, f1)
                m0 = jnp.where(pick_row, extra, m0)
                m1 = jnp.where(sub == 0, r1, f0)
                mirrored[0].append(m0)
                mirrored[1].append(m1)
            for h in range(2):
                rev = reverse_lanes(mirrored[h])
                for a in range(4):
                    cols = pl.ds(128 * a, 128)
                    own = spec_v[q, ky, pl.ds(8 * h, 8), cols]
                    if h == 0:
                        own = jnp.where(pick_own, spec_v[q, ky, pl.ds(16, 8), cols], own)
                    amp[q, ky, pl.ds(8 * h, 8), cols] = own + rev[a]

        @pl.when(p == 8)
        def _():
            @pl.loop(0, 32)
            def _(n):
                q = n // 16
                ky = lax.rem(n, 16)
                kr = lax.rem(16 - ky, 16)
                own_r, zero_r = [], []
                for a in range(4):
                    cols = pl.ds(128 * a, 128)
                    own_r.append(spec_v[q, kr, pl.ds(0, 8), cols])
                    zero_r.append(jnp.broadcast_to(row0r[16 * q + kr, :, cols], (8, 128)))
                own_r = reverse_lanes(own_r)
                zero_r = reverse_lanes(zero_r)
                for a in range(4):
                    cols = pl.ds(128 * a, 128)
                    last = spec_v[q, ky, pl.ds(0, 8), cols] + own_r[a]
                    first = jnp.broadcast_to(row0r[16 * q + ky, :, cols], (8, 128)) + zero_r[a]
                    old = amp[q, ky, pl.ds(0, 8), cols]
                    amp[q, ky, pl.ds(0, 8), cols] = jnp.where(sub == 0, 0.25 * (first + last), old)
                    bmp[q, ky, :, cols] = jnp.where(sub == 0, 0.25 * (first - last), 0.0)

    def y_stage(re, im, weight, store):
        re, im = fft16(re, im, -1)
        for q in range(2):
            wr, wi = [], []
            for ky in range(16):
                m = weight(q, ky)
                wr.append(m * re[ky])
                wi.append(m * im[ky])
            wr, wi = fft16(wr, wi, 1)
            for y in range(16):
                store(q, 0, y, wr[y])
                store(q, 1, y, wi[y])

    def wait_bytes(ref, sem):
        pltpu.make_async_copy(ref, ref, sem).wait()

    @pl.loop(0, WAVE_STEPS)
    def _(step):
        b = split(cur[...])
        b = tuple(jnp.concatenate([v, v], axis=0) for v in b)
        out = dot3((zt[0], zt[1]), b, 1, 1).reshape(2, NP, 2, 8, 128)
        wide = lax.broadcasted_iota(jnp.int32, (NP, 8, 128), 2)
        for h in range(2):
            fsend[:, pl.ds(8 * h, 8), :] = jnp.where(wide < 64, out[h, :, 0], out[h, :, 1])

        @pl.loop(1, NP)
        def _(o):
            d = lax.rem(p + o, NP)
            remote(fsend.at[d], frecv.at[step, p], fs.at[0], fr.at[step], (t, d)).start()

        frecv[step, p] = fsend[p]
        wait_bytes(frecv.at[step, pl.ds(0, NP - 1)], fr.at[step])

        groups = [exchange_groups([frecv[step, 8 * a + i] for i in range(8)]) for a in range(2)]
        parts = []
        for c in range(2):
            rows = [
                jnp.concatenate(
                    [groups[0][y * 2 + c], groups[1][y * 2 + c], groups[0][4 + y * 2 + c], groups[1][4 + y * 2 + c]],
                    axis=1,
                )
                for y in range(2)
            ]
            lhs = split(jnp.concatenate(rows, axis=0))
            parts.append(dot3(lhs, (xt[c, 0], xt[c, 1]), 1, 1))
        for lo, v in ((0, parts[0] + parts[1]), (256, parts[0] - parts[1])):
            for h in range(2):
                for y in range(2):
                    for ri in range(2):
                        vsend[h, y, ri, :, pl.ds(lo, 256)] = v[
                            y * 16 + 8 * h : y * 16 + 8 * h + 8, ri * 256 : ri * 256 + 256
                        ]
        wait_bytes(fsend.at[pl.ds(0, NP - 1)], fs.at[0])

        for h in range(2):

            @pl.loop(1, NT)
            def _(o):
                d = lax.rem(t + o, NT)
                remote(vsend.at[h], agb.at[step, h, t], gs.at[h], gr.at[step, h], (d, p)).start()

            agb[step, h, t] = vsend[h]

        @pl.when(step == 0)
        def _():
            build_amp()
            loads[5].wait()
            @pl.loop(0, 8)
            def _(n):
                q = n // 4
                cols = pl.ds(pl.multiple_of(lax.rem(n, 4) * 128, 128), 128)
                for y in range(NY):
                    rows = loc_v[q, :, y, cols]
                    for c in range(2):
                        index = (2 * sub + c) % 8
                        for i in range(2):
                            pair = [
                                jnp.take_along_axis(rows[16 * i + 8 * j : 16 * i + 8 * j + 8], index, axis=0)
                                for j in range(2)
                            ]
                            lr[q, y, pl.ds(16 * c + 8 * i, 8), cols] = jnp.where(sub < 4, pair[0], pair[1])

        for h in range(2):
            wait_bytes(agb.at[step, h, pl.ds(0, NT - 1)], gr.at[step, h])

            @pl.loop(0, 4)
            def _(a):
                cols = pl.ds(pl.multiple_of(a * 128, 128), 128)

                def weight(q, ky):
                    return amp[q, ky, pl.ds(8 * h, 8), cols]

                def store(q, ri, y, value):
                    w[q, ri, y, :, cols] = value

                y_stage(
                    [agb[step, h, y // 2, y % 2, 0, :, cols] for y in range(16)],
                    [agb[step, h, y // 2, y % 2, 1, :, cols] for y in range(16)],
                    weight,
                    store,
                )

            if h == 0:

                @pl.when(p == 8)
                def _():
                    @pl.loop(0, 4)
                    def _(a):
                        cols = pl.ds(pl.multiple_of(a * 128, 128), 128)
                        far = pl.ds(pl.multiple_of((3 - a) * 128, 128), 128)
                        near = pl.ds(pl.multiple_of(lax.rem(4 - a, 4) * 128, 128), 128)
                        index = (128 - lane) % 128

                        def load(y, ri):
                            v0 = jnp.take_along_axis(agb[step, 0, y // 2, y % 2, ri, :, near], index, axis=1)
                            v1 = jnp.take_along_axis(agb[step, 0, y // 2, y % 2, ri, :, far], index, axis=1)
                            return jnp.where(lane == 0, v0, v1)

                        def weight(q, ky):
                            return bmp[q, ky, :, cols]

                        def store(q, ri, y, value):
                            w[q, ri, y, :, cols] += value

                        y_stage(
                            [load(y, 0) for y in range(16)],
                            [-load(y, 1) for y in range(16)],
                            weight,
                            store,
                        )

            @pl.loop(0, 2)
            def _(q):
                low = [w[q, ri, :, :, pl.ds(0, 256)].reshape(128, 256) for ri in range(2)]
                high = [w[q, ri, :, :, pl.ds(256, 256)].reshape(128, 256) for ri in range(2)]
                for c in range(2):
                    mix = [(lo + hi) if c == 0 else (lo - hi) for lo, hi in zip(low, high)]
                    lhs = split(jnp.concatenate(mix, axis=1))
                    xo[c] = dot3(lhs, (xt[c, 0], xt[c, 1]), 1, 0).reshape(16, 8, 512)

                @pl.loop(0, 16)
                def _(n):
                    yh = n // 4
                    ra = lax.rem(n, 4)
                    ri = ra // 2
                    first = 8 * lax.rem(ra, 2)
                    cols = pl.ds(pl.multiple_of(ra * 128, 128), 128)
                    tiles = exchange_groups([xo[i % 2, 4 * yh + i // 2, :, cols] for i in range(8)])
                    for i in range(8):
                        snd[h, first + i, yh, q, ri] = tiles[i]

            if h == 0:

                @pl.loop(1, NP)
                def _(o):
                    d = lax.rem(p + o, NP)
                    remote(snd.at[0, d], rcv.at[step, 0, p], as0.at[0], ar0.at[step], (t, d)).start()

            else:

                @pl.loop(0, 4)
                def _(i):
                    yh = lax.rem(t // 2 + 1 + i, 4)

                    @pl.loop(1, NP)
                    def _(o):
                        d = lax.rem(p + o, NP)
                        remote(
                            snd.at[1, d, yh], rcv.at[step, 1, p, yh], as1.at[0], ar1.at[step, yh], (t, d)
                        ).start()

            rcv[step, h, p] = snd[h, p]

        for h in range(2):
            wait_bytes(agb.at[step, h, pl.ds(0, NT - 1)], gs.at[h])

        wait_bytes(rcv.at[step, 0, pl.ds(0, NP - 1)], ar0.at[step])

        @pl.loop(0, 4)
        def _(i):
            yh = lax.rem(t // 2 + 1 + i, 4)
            wait_bytes(rcv.at[step, 1, pl.ds(0, NP - 1), yh], ar1.at[step, yh])
            total = None
            for q in range(2):
                d = jnp.concatenate(
                    [rcv[step, h, :, yh, q].reshape(256, 128) for h in range(2)], axis=0
                )
                field = dot3(split(d), (zt[0], zt[1]), 0, 0)
                field = field * lr[q, pl.ds(4 * yh, 4)].reshape(128, 512)
                total = field if total is None else total + field
            psend[pl.ds(2 * yh, 2)] = total.reshape(2, 64, 512)
            for j in range(2):
                d = 2 * yh + j

                @pl.when(d != t)
                def _():
                    remote(psend.at[d], rsr.at[step, t], rs.at[0], rr.at[step], (d, p)).start()

        wait_bytes(snd.at[0, pl.ds(0, NP - 1)], as0.at[0])
        wait_bytes(snd.at[1, pl.ds(0, NP - 1)], as1.at[0])
        rsr[step, t] = psend[t]
        wait_bytes(rsr.at[step, pl.ds(0, NT - 1)], rr.at[step])
        wait_bytes(psend.at[pl.ds(0, NT - 1)], rs.at[0])
        total = rsr[step, 0]
        for i in range(1, NT):
            total = total + rsr[step, i]
        advanced = SCALE * total - prev[...]
        dose[...] = dose[...] + advanced * advanced
        prev[...] = cur[...]
        cur[...] = advanced

    for y in range(2):
        for x in range(XR):
            row = y * XR + (x % 2) * 16 + x // 2
            final_o[x, pl.ds(y, 1), :] = cur[pl.ds(row, 1), :]
            dose_o[x, pl.ds(y, 1), :] = dose[pl.ds(row, 1), :]


def wave(pres, prior, loc, spec):
    brick = jax.ShapeDtypeStruct((XR, 2, NZ), F32)
    any_spec = pl.BlockSpec(memory_space=pl.ANY)
    vmem_spec = pl.BlockSpec(memory_space=pltpu.VMEM)
    scratch = [
        pltpu.VMEM((XR, NY, NZ), F32),
        pltpu.VMEM((XR, NY, NZ), F32),
        pltpu.VMEM((2, XR, NY, NZ), F32),
        pltpu.VMEM((2, NY, XR, NZ), F32),
        pltpu.VMEM((2, NY, 32, NX), F32),
        pltpu.VMEM((2, NY, 16, NX), F32),
        pltpu.VMEM((32, 1, NX), F32),
        pltpu.VMEM((32, 1, NX), F32),
        pltpu.VMEM((2, NY, 16, NX), F32),
        pltpu.VMEM((2, NY, 8, NX), F32),
        pltpu.VMEM((2, NZ, NZ), BF16),
        pltpu.VMEM((2, 2, NX, NX), BF16),
        pltpu.VMEM((64, NZ), F32),
        pltpu.VMEM((64, NZ), F32),
        pltpu.VMEM((64, NZ), F32),
        pltpu.VMEM((NP, 16, 128), F32),
        pltpu.VMEM((2, NP, 16, 128), F32),
        pltpu.VMEM((2, 2, 2, 8, NX), F32),
        pltpu.VMEM((2, 2, NT, 2, 2, 8, NX), F32),
        pltpu.VMEM((2, 2, NY, 8, NX), F32),
        pltpu.VMEM((2, NY, 8, NX), F32),
        pltpu.VMEM((2, NP, 4, 2, 2, 8, 128), F32),
        pltpu.VMEM((2, 2, NP, 4, 2, 2, 8, 128), F32),
        pltpu.VMEM((NT, 64, NZ), F32),
        pltpu.VMEM((2, NT, 64, NZ), F32),
        pltpu.SemaphoreType.DMA((6,)),
        pltpu.SemaphoreType.DMA((1,)),
        pltpu.SemaphoreType.DMA((4,)),
        pltpu.SemaphoreType.DMA((1,)),
        pltpu.SemaphoreType.DMA((2,)),
        pltpu.SemaphoreType.DMA((2,)),
        pltpu.SemaphoreType.DMA((2, 2)),
        pltpu.SemaphoreType.DMA((1,)),
        pltpu.SemaphoreType.DMA((2,)),
        pltpu.SemaphoreType.DMA((1,)),
        pltpu.SemaphoreType.DMA((2, 4)),
        pltpu.SemaphoreType.DMA((1,)),
        pltpu.SemaphoreType.DMA((2,)),
    ]
    return pl.pallas_call(
        wave_kernel,
        name="wave",
        out_shape=(brick, brick),
        in_specs=[any_spec] * 6,
        out_specs=(vmem_spec, vmem_spec),
        scratch_shapes=scratch,
        compiler_params=pltpu.CompilerParams(
            collective_id=0, has_side_effects=True, vmem_limit_bytes=60 * 2**20
        ),
    )(pres, prior, loc, spec, jnp.asarray(z_table()), jnp.asarray(x_table()))


def padded_2(block, sides, width):
    for axis, dim in sides:
        count = lax.axis_size(axis)
        forward = [(i, i + 1) for i in range(count - 1)]
        backward = [(target, source) for source, target in forward]
        low = lax.ppermute(
            lax.slice_in_dim(block, block.shape[dim] - width, None, axis=dim), axis, forward
        )
        high = lax.ppermute(lax.slice_in_dim(block, 0, width, axis=dim), axis, backward)
        block = jnp.concatenate([low, block, high], axis=dim)
    return block


def stencil_sum(padded):
    center = padded[1:-1, 1:-1, :]
    depth_pad = jnp.pad(center, ((0, 0), (0, 0), (1, 1)))
    near_sum = padded[2:, 1:-1, :] + padded[:-2, 1:-1, :]
    near_sum = near_sum + padded[1:-1, 2:, :] + padded[1:-1, :-2, :]
    near_sum = near_sum + depth_pad[:, :, 2:] + depth_pad[:, :, :-2]
    return (center, near_sum)


def heat_update(center, near_sum, perfuse, source):
    return center + DIFFUSION * (near_sum - 6.0 * center) - perfuse * center + source


def on_device(
    present_acoustic,
    prior_acoustic,
    location_factor,
    spectral_multiplier,
    medium_kinds,
    organ_properties,
    thermal_increase,
):
    final_brick, dose_sum = wave(present_acoustic, prior_acoustic, location_factor, spectral_multiplier)
    absorb = jnp.where(
        medium_kinds == 0,
        organ_properties[0, 0],
        jnp.where(medium_kinds == 1, organ_properties[1, 0], organ_properties[2, 0]),
    )
    perfuse = jnp.where(
        medium_kinds == 0,
        organ_properties[0, 1],
        jnp.where(medium_kinds == 1, organ_properties[1, 1], organ_properties[2, 1]),
    )
    source = absorb * dose_sum
    present_thermal = thermal_increase
    for _ in range(HEAT_STEPS):
        padded = padded_2(present_thermal, (("term", 1), ("pencil", 0)), 1)
        center, near_sum = stencil_sum(padded)
        present_thermal = heat_update(center, near_sum, perfuse, source)
    return (final_brick, present_thermal)


def solution(mesh):
    return jax.shard_map(
        on_device,
        mesh=mesh,
        in_specs=(
            P("pencil", None, None),
            P("pencil", None, None),
            P("term", "pencil", None, None),
            P("term", None, "pencil", None),
            P("pencil", "term", None),
            P(),
            P("pencil", "term", None),
        ),
        out_specs=(P("pencil", "term", None), P("pencil", "term", None)),
        check_vma=False,
    )
```

time: 934 us -> 206 us (0.22)
  local copies, waits for them, and re-layouts: 242 us -> 4.33 us
  matrix products: 224 us -> 0 us
  waiting for transfers between devices: 186 us -> 7.51 us
  Pallas kernels: 0 us -> 152 us
  blocking collectives: 132 us -> 0 us
  other arithmetic: 78.9 us -> 12 us
  starting transfers between devices: 43.5 us -> 26.3 us
  between operations: 15.3 us -> 0.78 us
    dot_general x40 -> x0, matrix products: 224 us -> none  [the longest x16 124 us: matmul(): jnp.dot(left, right, precision=lax.Precision.HIGHEST, preferred_element_t...]
    pallas_call x0 -> x1, Pallas kernels: none -> 152 us  [wave(): pl.pallas_call(wave_kernel, name='wave', out_shape=(brick, brick), in_spe...]
    all_to_all x3 -> x0, blocking collectives: 132 us -> none  [the longest x2 75.8 us: on_device(): lax.all_to_all(rows_spec, 'pencil', split_axis=2, concat_axis=3, tiled=True)]
    psum x2 -> x0, waiting for transfers between devices: 131 us -> none  [on_device(): summed = lax.psum(partial_value, 'term')]
    unnamed x42 -> x5, local copies, waits for them, and re-layouts: 93.7 us -> 1.57 us
    all_to_all x7 -> x0, local copies, waits for them, and re-layouts: 78.7 us -> none  [the longest x4 61.7 us: on_device(): lax.all_to_all(term_restored, 'pencil', split_axis=4, concat_axis=3, tile...]
    all_to_all x1 -> x0, waiting for transfers between devices: 52.4 us -> none  [on_device(): lax.all_to_all(term_restored, 'pencil', split_axis=4, concat_axis=3, tile...]
    another operation x6 -> x0, local copies, waits for them, and re-layouts: 45.7 us -> none  [the longest x4 30.4 us: inverse_columns(): jnp.stack([real_part.reshape(inner_shape), imag_part.reshape(inner_shape)...]
  transfers between devices with their start and end apart: 11 -> 8, of which waited for: 6 -> 3; matrix products, arithmetic and copies ran while one was open for 0% -> 1% of each run, Pallas kernels for 0% -> 75%
where the time goes in v1:
time: 206 us; the launch traced here: 203 us
  Pallas kernels  152 us (74%)
  starting transfers between devices  26.3 us (13%)
  other arithmetic  12 us (6%)
  waiting for transfers between devices  7.51 us (4%)
  local copies, waits for them, and re-layouts  4.33 us (2%)
    pallas_call x1, Pallas kernels, wave(): pl.pallas_call(wave_kernel, name='wave', out_shape=(brick, brick), in_spe...  152 us
    ppermute x4, starting transfers between devices, padded_2(): lax.ppermute(lax.slice_in_dim(block, 0, width, axis=dim), axis, backward)  13.9 us
    ppermute x4, starting transfers between devices, padded_2(): lax.ppermute(lax.slice_in_dim(block, block.shape[dim] - width, None, axis...  12.4 us
    add x2, other arithmetic, heat_update(): center + DIFFUSION * (near_sum - 6.0 * center) - perfuse * center + source  11.2 us
    ppermute x4, waiting for transfers between devices, padded_2(): lax.ppermute(lax.slice_in_dim(block, block.shape[dim] - width, None, axis...  7.5 us
  transfers between devices with their start and end apart: 8, of which 3 were waited for; matrix products, arithmetic and copies ran while one was open for 1% of the time, Pallas kernels for 75%

profile of v1, /device:TPU:33, one launch (start us, length us, event | category | flops | bytes accessed | tf_op | source)
XLA Modules:
  0.0 203.0 jit_solution(18183492046124019088)
XLA Ops:
  0.6 1.1 fusion.13
  1.7 2.7 %collective-permute-start.1 = (f32[32,1,512]{2,1,0:T(1,128)S(1)}, f32[32,1,512]{2,1,0:T(1,128)S(1)}, u32[]{:S(2)}, u32[]{:S(2)}) collective-permute-start(f32[32,1,512]{2,1,0:T(1,128)S(1)} %get-tuple-element.12), channel_id=1, source_target_pairs={{16,0},{32,16},{48,32},{64,48},{80,64},{96,80},{112,96},{17,1},{33... | collective-permute-start | bytes 196616 | tf_op jit(solution)/shard_map/ppermute | solution.py:547
  4.5 2.5 %collective-permute-start = (f32[32,1,512]{2,1,0:T(1,128)S(1)}, f32[32,1,512]{2,1,0:T(1,128)S(1)}, u32[]{:S(2)}, u32[]{:S(2)}) collective-permute-start(f32[32,1,512]{2,1,0:T(1,128)S(1)} %get-tuple-element.13), channel_id=1, source_target_pairs={{0,16},{16,32},{32,48},{48,64},{64,80},{80,96},{96,112},{1,17},{17... | collective-permute-start | bytes 196616 | tf_op jit(solution)/shard_map/ppermute | solution.py:544
  7.0 0.0 collective-permute-done.1
  7.0 3.4 %collective-permute-done = f32[32,1,512]{2,1,0:T(1,128)S(1)} collective-permute-done((f32[32,1,512]{2,1,0:T(1,128)S(1)}, f32[32,1,512]{2,1,0:T(1,128)S(1)}, u32[]{:S(2)}, u32[]{:S(2)}) %collective-permute-start) | collective-permute-done | bytes 65568 | tf_op jit(solution)/shard_map/ppermute | solution.py:544
  10.4 0.7 pad_maximum_fusion.21
  11.1 4.0 %collective-permute-start.2 = (f32[1,4,512]{2,1,0:T(4,128)S(1)}, f32[1,4,512]{2,1,0:T(4,128)S(1)}, u32[]{:S(2)}, u32[]{:S(2)}) collective-permute-start(f32[1,4,512]{2,1,0:T(4,128)S(1)} %get-tuple-element.8), channel_id=1, source_target_pairs={{1,0},{2,1},{3,2},{4,3},{5,4},{6,5},{7,6},{8,7},{9,8},{10,9},{11,1... | collective-permute-start | bytes 24584 | tf_op jit(solution)/shard_map/ppermute | solution.py:547
  15.1 4.4 %collective-permute-start.3 = (f32[1,4,512]{2,1,0:T(4,128)S(1)}, f32[1,4,512]{2,1,0:T(4,128)S(1)}, u32[]{:S(2)}, u32[]{:S(2)}) collective-permute-start(f32[1,4,512]{2,1,0:T(4,128)S(1)} %get-tuple-element.9), channel_id=1, source_target_pairs={{0,1},{1,2},{2,3},{3,4},{4,5},{5,6},{6,7},{7,8},{8,9},{9,10},{10,1... | collective-permute-start | bytes 24584 | tf_op jit(solution)/shard_map/ppermute | solution.py:544
  19.6 1.6 fusion.14
  21.1 0.0 copy-start
  21.1 0.0 copy-start.1
  21.1 152.2 %wave.1 = (f32[32,2,512]{2,1,0:T(2,128)}, f32[32,2,512]{2,1,0:T(2,128)}) custom-call(f32[32,16,512]{2,1,0:T(8,128)} %pres.1, f32[32,16,512]{2,1,0:T(8,128)} %prior.1, f32[2,32,16,512]{3,2,1,0:T(8,128)} %loc.1, f32[2,16,32,512]{3,2,1,0:T(8,128)} %spec.1, bf16[2,512,512]{2,1,0:T(8,128)(2,1)} %constant.15.clone.ztab, bf16[2,2,512,512]{3,2,1,0:T(8,128)(2,1)} %constant.16.clone.xtab), custom_call_target="tpu_custom_call" | custom-call | tf_op jit(solution)/shard_map/wave/pallas_call | solution.py:526
  173.3 0.0 collective-permute-done.2
  173.3 0.0 collective-permute-done.3
  173.3 0.0 copy-done
  173.3 0.0 copy-done.1
  173.3 5.3 %subtract_add_fusion.1 = f32[32,2,512]{2,1,0:T(2,128)S(1)} fusion(f32[32,2,512]{2,1,0:T(2,128)S(1)} %copy-done, f32[32,1,512]{2,1,0:T(1,128)S(1)} %collective-permute-done, f32[32,1,512]{2,1,0:T(1,128)S(1)} %collective-permute-done.1, f32[1,4,512]{2,1,0:T(4,128)S(1)} %collective-permute-done.3, f32[1,4,512]{2,1,0:T(4,128)S(1)} %collective-permute-done.2, ...), kind=kLoop, calls=%fused_computation.34 | loop fusion | flops 884736 | bytes 671768 | tf_op jit(solution)/shard_map/add | solution.py:562
  178.6 0.1 fusion.12
  178.7 2.8 %collective-permute-start.5 = (f32[32,1,512]{2,1,0:T(1,128)S(1)}, f32[32,1,512]{2,1,0:T(1,128)S(1)}, u32[]{:S(2)}, u32[]{:S(2)}) collective-permute-start(f32[32,1,512]{2,1,0:T(1,128)S(1)} %get-tuple-element.10), channel_id=1, source_target_pairs={{16,0},{32,16},{48,32},{64,48},{80,64},{96,80},{112,96},{17,1},{33... | collective-permute-start | bytes 196616 | tf_op jit(solution)/shard_map/ppermute | solution.py:547
  181.5 2.5 %collective-permute-start.4 = (f32[32,1,512]{2,1,0:T(1,128)S(1)}, f32[32,1,512]{2,1,0:T(1,128)S(1)}, u32[]{:S(2)}, u32[]{:S(2)}) collective-permute-start(f32[32,1,512]{2,1,0:T(1,128)S(1)} %get-tuple-element.11), channel_id=1, source_target_pairs={{0,16},{16,32},{32,48},{48,64},{64,80},{80,96},{96,112},{1,17},{17... | collective-permute-start | bytes 196616 | tf_op jit(solution)/shard_map/ppermute | solution.py:544
  184.0 0.0 collective-permute-done.5
  184.0 3.4 %collective-permute-done.4 = f32[32,1,512]{2,1,0:T(1,128)S(1)} collective-permute-done((f32[32,1,512]{2,1,0:T(1,128)S(1)}, f32[32,1,512]{2,1,0:T(1,128)S(1)}, u32[]{:S(2)}, u32[]{:S(2)}) %collective-permute-start.4) | collective-permute-done | bytes 65568 | tf_op jit(solution)/shard_map/ppermute | solution.py:544
  187.4 4.4 %collective-permute-start.6 = (f32[1,4,512]{2,1,0:T(4,128)S(1)}, f32[1,4,512]{2,1,0:T(4,128)S(1)}, u32[]{:S(2)}, u32[]{:S(2)}) collective-permute-start(f32[1,4,512]{2,1,0:T(4,128)S(1)} %get-tuple-element.6), channel_id=1, source_target_pairs={{1,0},{2,1},{3,2},{4,3},{5,4},{6,5},{7,6},{8,7},{9,8},{10,9},{11,1... | collective-permute-start | bytes 24584 | tf_op jit(solution)/shard_map/ppermute | solution.py:547
  191.8 2.9 %collective-permute-start.7 = (f32[1,4,512]{2,1,0:T(4,128)S(1)}, f32[1,4,512]{2,1,0:T(4,128)S(1)}, u32[]{:S(2)}, u32[]{:S(2)}) collective-permute-start(f32[1,4,512]{2,1,0:T(4,128)S(1)} %get-tuple-element.7), channel_id=1, source_target_pairs={{0,1},{1,2},{2,3},{3,4},{4,5},{5,6},{6,7},{7,8},{8,9},{9,10},{10,1... | collective-permute-start | bytes 24584 | tf_op jit(solution)/shard_map/ppermute | solution.py:544
  194.8 0.0 collective-permute-done.6
  194.8 0.8 collective-permute-done.7
  195.5 5.9 %subtract_add_fusion = f32[32,2,512]{2,1,0:T(2,128)} fusion(f32[32,2,512]{2,1,0:T(2,128)S(1)} %subtract_add_fusion.1, f32[32,1,512]{2,1,0:T(1,128)S(1)} %collective-permute-done.4, f32[32,1,512]{2,1,0:T(1,128)S(1)} %collective-permute-done.5, f32[1,4,512]{2,1,0:T(4,128)S(1)} %collective-permute-done.7, f32[1,4,512]{2,1,0:T(4,128)S(1)} %collective-permute-done.6, ...), kind=kLoop, calls=%fused_computation.32 | loop fusion | flops 884736 | bytes 671768 | tf_op jit(solution)/shard_map/add | solution.py:562
  201.5 1.6 copy.12
  (1 shorter events, 0.0 us)
Async XLA Ops:
  1.7 5.3 %collective-permute-start.1 = (f32[32,1,512]{2,1,0:T(1,128)S(1)}, f32[32,1,512]{2,1,0:T(1,128)S(1)}, u32[]{:S(2)}, u32[]{:S(2)}) collective-permute-start(f32[32,1,512]{2,1,0:T(1,128)S(1)} %get-tuple-element.12), channel_id=1, source_target_pairs={{16,0},{32,16},{48,32},{64,48},{80,64},{96,80},{112,96},{17,1},{33... | collective-permute-start | bytes 196616 | tf_op jit(solution)/shard_map/ppermute | solution.py:547
  4.5 5.9 %collective-permute-start = (f32[32,1,512]{2,1,0:T(1,128)S(1)}, f32[32,1,512]{2,1,0:T(1,128)S(1)}, u32[]{:S(2)}, u32[]{:S(2)}) collective-permute-start(f32[32,1,512]{2,1,0:T(1,128)S(1)} %get-tuple-element.13), channel_id=1, source_target_pairs={{0,16},{16,32},{32,48},{48,64},{64,80},{80,96},{96,112},{1,17},{17... | collective-permute-start | bytes 196616 | tf_op jit(solution)/shard_map/ppermute | solution.py:544
  11.1 162.2 %collective-permute-start.2 = (f32[1,4,512]{2,1,0:T(4,128)S(1)}, f32[1,4,512]{2,1,0:T(4,128)S(1)}, u32[]{:S(2)}, u32[]{:S(2)}) collective-permute-start(f32[1,4,512]{2,1,0:T(4,128)S(1)} %get-tuple-element.8), channel_id=1, source_target_pairs={{1,0},{2,1},{3,2},{4,3},{5,4},{6,5},{7,6},{8,7},{9,8},{10,9},{11,1... | collective-permute-start | bytes 24584 | tf_op jit(solution)/shard_map/ppermute | solution.py:547
  15.1 158.2 %collective-permute-start.3 = (f32[1,4,512]{2,1,0:T(4,128)S(1)}, f32[1,4,512]{2,1,0:T(4,128)S(1)}, u32[]{:S(2)}, u32[]{:S(2)}) collective-permute-start(f32[1,4,512]{2,1,0:T(4,128)S(1)} %get-tuple-element.9), channel_id=1, source_target_pairs={{0,1},{1,2},{2,3},{3,4},{4,5},{5,6},{6,7},{7,8},{8,9},{9,10},{10,1... | collective-permute-start | bytes 24584 | tf_op jit(solution)/shard_map/ppermute | solution.py:544
  21.1 152.2 %copy-start = (f32[32,2,512]{2,1,0:T(2,128)S(1)}, f32[32,2,512]{2,1,0:T(2,128)}, u32[]{:S(2)}) copy-start(f32[32,2,512]{2,1,0:T(2,128)} %param.15) | copy-start | bytes 393220
  21.1 152.2 %copy-start.1 = (s32[32,2,512]{2,1,0:T(2,128)S(1)}, s32[32,2,512]{2,1,0:T(2,128)}, u32[]{:S(2)}) copy-start(s32[32,2,512]{2,1,0:T(2,128)} %param.13) | copy-start | bytes 393220
  178.7 5.3 %collective-permute-start.5 = (f32[32,1,512]{2,1,0:T(1,128)S(1)}, f32[32,1,512]{2,1,0:T(1,128)S(1)}, u32[]{:S(2)}, u32[]{:S(2)}) collective-permute-start(f32[32,1,512]{2,1,0:T(1,128)S(1)} %get-tuple-element.10), channel_id=1, source_target_pairs={{16,0},{32,16},{48,32},{64,48},{80,64},{96,80},{112,96},{17,1},{33... | collective-permute-start | bytes 196616 | tf_op jit(solution)/shard_map/ppermute | solution.py:547
  181.5 5.9 %collective-permute-start.4 = (f32[32,1,512]{2,1,0:T(1,128)S(1)}, f32[32,1,512]{2,1,0:T(1,128)S(1)}, u32[]{:S(2)}, u32[]{:S(2)}) collective-permute-start(f32[32,1,512]{2,1,0:T(1,128)S(1)} %get-tuple-element.11), channel_id=1, source_target_pairs={{0,16},{16,32},{32,48},{48,64},{64,80},{80,96},{96,112},{1,17},{17... | collective-permute-start | bytes 196616 | tf_op jit(solution)/shard_map/ppermute | solution.py:544
  187.4 7.3 %collective-permute-start.6 = (f32[1,4,512]{2,1,0:T(4,128)S(1)}, f32[1,4,512]{2,1,0:T(4,128)S(1)}, u32[]{:S(2)}, u32[]{:S(2)}) collective-permute-start(f32[1,4,512]{2,1,0:T(4,128)S(1)} %get-tuple-element.6), channel_id=1, source_target_pairs={{1,0},{2,1},{3,2},{4,3},{5,4},{6,5},{7,6},{8,7},{9,8},{10,9},{11,1... | collective-permute-start | bytes 24584 | tf_op jit(solution)/shard_map/ppermute | solution.py:547
  191.8 3.7 %collective-permute-start.7 = (f32[1,4,512]{2,1,0:T(4,128)S(1)}, f32[1,4,512]{2,1,0:T(4,128)S(1)}, u32[]{:S(2)}, u32[]{:S(2)}) collective-permute-start(f32[1,4,512]{2,1,0:T(4,128)S(1)} %get-tuple-element.7), channel_id=1, source_target_pairs={{0,1},{1,2},{2,3},{3,4},{4,5},{5,6},{6,7},{7,8},{8,9},{9,10},{10,1... | collective-permute-start | bytes 24584 | tf_op jit(solution)/shard_map/ppermute | solution.py:544

commit v2 on v1

--- a/solution.py
+++ b/solution.py
@@ -10,7 +10,6 @@
 from jax.sharding import PartitionSpec as P
 
 WAVE_STEPS = 2
-HEAT_STEPS = 2
 DIFFUSION = 0.125
 MESH = pl.DeviceIdType.MESH
 F32 = jnp.float32
@@ -131,10 +130,11 @@
 
 
 def wave_kernel(
-    pres, prior, loc, spec, ztab, xtab, final_o, dose_o,
+    pres, prior, loc, spec, ztab, xtab, kinds, thermal, props, final_o, heat_o,
     pres_v, prior_v, loc_v, lr, spec_v, srecv, row0, row0r, amp, bmp, zt, xt,
+    kind_v, heat_v, absorb, perfuse, heat, field, hxs, hx, hy,
     cur, prev, dose, fsend, frecv, vsend, agb, w, xo, snd, rcv, psend, rsr,
-    lsem, ssem, sx, fs, fr, gs, gr, as0, ar0, as1, ar1, rs, rr,
+    lsem, ssem, sx, fs, fr, gs, gr, as0, ar0, as1, ar1, rs, rr, hs, hr,
 ):
     t = lax.axis_index("term")
     p = lax.axis_index("pencil")
@@ -152,7 +152,7 @@
     loads = [
         pltpu.make_async_copy(src, dst, lsem.at[i])
         for i, (src, dst) in enumerate(
-            [(pres, pres_v), (ztab, zt), (xtab, xt), (spec, spec_v), (prior, prior_v), (loc, loc_v)]
+            [(pres, pres_v), (ztab, zt), (xtab, xt), (spec, spec_v), (prior, prior_v), (loc, loc_v), (kinds, kind_v), (thermal, heat_v)]
         )
     ]
     for load in loads:
@@ -196,6 +196,99 @@
     lane = lax.broadcasted_iota(jnp.int32, (8, 128), 1)
     sub = lax.broadcasted_iota(jnp.int32, (8, 128), 0)
     flip = (8 - sub) % 8
+
+    edges = [
+        (t > 0, (t - 1, p)),
+        (t < NT - 1, (t + 1, p)),
+        (p > 0, (t, p - 1)),
+        (p < NP - 1, (t, p + 1)),
+    ]
+
+    def halo_copy(k, e):
+        if e < 2:
+            src, dst = field.at[k, pl.ds(32 * e, 32)], hy.at[k, 1 - e]
+        else:
+            src, dst = hxs.at[k, e - 2], hx.at[k, 3 - e]
+        return remote(src, dst, hs.at[k, e], hr.at[k, 1 - e if e < 2 else 5 - e], edges[e][1])
+
+    def halo_start(k):
+        for y in range(2):
+            hxs[k, 0, pl.ds(y, 1), :] = field[k, pl.ds(32 * y, 1), :]
+            hxs[k, 1, pl.ds(y, 1), :] = field[k, pl.ds(32 * y + 31, 1), :]
+        for e in range(4):
+
+            @pl.when(edges[e][0])
+            def _():
+                halo_copy(k, e).start()
+
+            @pl.when(jnp.logical_not(edges[e][0]))
+            def _():
+                if e < 2:
+                    hy[k, e] = jnp.zeros((32, NZ), F32)
+                else:
+                    hx[k, e - 2] = jnp.zeros((2, NZ), F32)
+
+    def halo_wait(k):
+        for e in range(4):
+
+            @pl.when(edges[e][0])
+            def _():
+                halo_copy(k, e).wait_send()
+                ref = hy.at[k, e] if e < 2 else hx.at[k, e - 2]
+                pltpu.make_async_copy(ref, ref, hr.at[k, e]).wait()
+
+    row16 = lax.broadcasted_iota(jnp.int32, (16, NZ), 0)
+    col16 = lax.broadcasted_iota(jnp.int32, (16, NZ), 1)
+
+    def heat_apply(k, y, c):
+        mine = field[k, pl.ds(32 * y + 16 * c, 16), :]
+        other = field[k, pl.ds(32 * y + 16 * (1 - c), 16), :]
+        if c == 0:
+            shifted = jnp.where(row16 == 0, hx[k, 0, pl.ds(y, 1), :], pltpu.roll(other, 1, 0))
+        else:
+            shifted = jnp.where(row16 == 15, hx[k, 1, pl.ds(y, 1), :], pltpu.roll(other, 15, 0))
+        near = other + shifted
+        near = near + field[k, pl.ds(32 * (1 - y) + 16 * c, 16), :] + hy[k, y, pl.ds(16 * c, 16), :]
+        near = near + jnp.where(col16 == 0, 0.0, pltpu.roll(mine, 1, 1))
+        near = near + jnp.where(col16 == NZ - 1, 0.0, pltpu.roll(mine, NZ - 1, 1))
+        rows = pl.ds(32 * y + 16 * c, 16)
+        return mine + DIFFUSION * (near - 6.0 * mine) - perfuse[rows, :] * mine
+
+    def heat_begin():
+        loads[6].wait()
+        loads[7].wait()
+        for y in range(2):
+            for x in range(XR):
+                row = y * XR + (x % 2) * 16 + x // 2
+                field[0, pl.ds(row, 1), :] = heat_v[x, pl.ds(y, 1), :]
+                kind = kind_v[x, pl.ds(y, 1), :]
+                for ref, j in ((absorb, 0), (perfuse, 1)):
+                    ref[pl.ds(row, 1), :] = jnp.where(
+                        kind == 0, props[0, j], jnp.where(kind == 1, props[1, j], props[2, j])
+                    )
+        halo_start(0)
+
+    def heat_middle():
+        halo_wait(0)
+        for y in range(2):
+            for c in range(2):
+                field[1, pl.ds(32 * y + 16 * c, 16), :] = heat_apply(0, y, c)
+        halo_start(1)
+
+    def heat_late():
+        halo_wait(1)
+        for y in range(2):
+            for c in range(2):
+                heat[pl.ds(32 * y + 16 * c, 16), :] = heat_apply(1, y, c)
+
+    def heat_finish():
+        field[2] = absorb[...] * dose[...]
+        halo_start(2)
+        halo_wait(2)
+        for y in range(2):
+            for c in range(2):
+                rows = pl.ds(32 * y + 16 * c, 16)
+                heat[rows, :] = heat[rows, :] + (field[2, rows, :] + heat_apply(2, y, c))
 
     def build_amp():
         swap.wait()
@@ -326,6 +419,9 @@
 
         @pl.when(step == 0)
         def _():
+            heat_begin()
+            heat_middle()
+            heat_late()
             build_amp()
             loads[5].wait()
             @pl.loop(0, 8)
@@ -472,14 +568,15 @@
         prev[...] = cur[...]
         cur[...] = advanced
 
+    heat_finish()
     for y in range(2):
         for x in range(XR):
             row = y * XR + (x % 2) * 16 + x // 2
             final_o[x, pl.ds(y, 1), :] = cur[pl.ds(row, 1), :]
-            dose_o[x, pl.ds(y, 1), :] = dose[pl.ds(row, 1), :]
-
-
-def wave(pres, prior, loc, spec):
+            heat_o[x, pl.ds(y, 1), :] = heat[pl.ds(row, 1), :]
+
+
+def wave(pres, prior, loc, spec, kinds, props, thermal):
     brick = jax.ShapeDtypeStruct((XR, 2, NZ), F32)
     any_spec = pl.BlockSpec(memory_space=pl.ANY)
     vmem_spec = pl.BlockSpec(memory_space=pltpu.VMEM)
@@ -496,6 +593,15 @@
         pltpu.VMEM((2, NY, 8, NX), F32),
         pltpu.VMEM((2, NZ, NZ), BF16),
         pltpu.VMEM((2, 2, NX, NX), BF16),
+        pltpu.VMEM((XR, 2, NZ), jnp.int32),
+        pltpu.VMEM((XR, 2, NZ), F32),
+        pltpu.VMEM((64, NZ), F32),
+        pltpu.VMEM((64, NZ), F32),
+        pltpu.VMEM((64, NZ), F32),
+        pltpu.VMEM((3, 64, NZ), F32),
+        pltpu.VMEM((3, 2, 2, NZ), F32),
+        pltpu.VMEM((3, 2, 2, NZ), F32),
+        pltpu.VMEM((3, 2, 32, NZ), F32),
         pltpu.VMEM((64, NZ), F32),
         pltpu.VMEM((64, NZ), F32),
         pltpu.VMEM((64, NZ), F32),
@@ -509,7 +615,7 @@
         pltpu.VMEM((2, 2, NP, 4, 2, 2, 8, 128), F32),
         pltpu.VMEM((NT, 64, NZ), F32),
         pltpu.VMEM((2, NT, 64, NZ), F32),
-        pltpu.SemaphoreType.DMA((6,)),
+        pltpu.SemaphoreType.DMA((8,)),
         pltpu.SemaphoreType.DMA((1,)),
         pltpu.SemaphoreType.DMA((4,)),
         pltpu.SemaphoreType.DMA((1,)),
@@ -522,78 +628,25 @@
         pltpu.SemaphoreType.DMA((2, 4)),
         pltpu.SemaphoreType.DMA((1,)),
         pltpu.SemaphoreType.DMA((2,)),
+        pltpu.SemaphoreType.DMA((3, 4)),
+        pltpu.SemaphoreType.DMA((3, 4)),
     ]
     return pl.pallas_call(
         wave_kernel,
         name="wave",
         out_shape=(brick, brick),
-        in_specs=[any_spec] * 6,
+        in_specs=[any_spec] * 8 + [pl.BlockSpec(memory_space=pltpu.SMEM)],
         out_specs=(vmem_spec, vmem_spec),
         scratch_shapes=scratch,
         compiler_params=pltpu.CompilerParams(
             collective_id=0, has_side_effects=True, vmem_limit_bytes=60 * 2**20
         ),
-    )(pres, prior, loc, spec, jnp.asarray(z_table()), jnp.asarray(x_table()))
-
-
-def padded_2(block, sides, width):
-    for axis, dim in sides:
-        count = lax.axis_size(axis)
-        forward = [(i, i + 1) for i in range(count - 1)]
-        backward = [(target, source) for source, target in forward]
-        low = lax.ppermute(
-            lax.slice_in_dim(block, block.shape[dim] - width, None, axis=dim), axis, forward
-        )
-        high = lax.ppermute(lax.slice_in_dim(block, 0, width, axis=dim), axis, backward)
-        block = jnp.concatenate([low, block, high], axis=dim)
-    return block
-
-
-def stencil_sum(padded):
-    center = padded[1:-1, 1:-1, :]
-    depth_pad = jnp.pad(center, ((0, 0), (0, 0), (1, 1)))
-    near_sum = padded[2:, 1:-1, :] + padded[:-2, 1:-1, :]
-    near_sum = near_sum + padded[1:-1, 2:, :] + padded[1:-1, :-2, :]
-    near_sum = near_sum + depth_pad[:, :, 2:] + depth_pad[:, :, :-2]
-    return (center, near_sum)
-
-
-def heat_update(center, near_sum, perfuse, source):
-    return center + DIFFUSION * (near_sum - 6.0 * center) - perfuse * center + source
-
-
-def on_device(
-    present_acoustic,
-    prior_acoustic,
-    location_factor,
-    spectral_multiplier,
-    medium_kinds,
-    organ_properties,
-    thermal_increase,
-):
-    final_brick, dose_sum = wave(present_acoustic, prior_acoustic, location_factor, spectral_multiplier)
-    absorb = jnp.where(
-        medium_kinds == 0,
-        organ_properties[0, 0],
-        jnp.where(medium_kinds == 1, organ_properties[1, 0], organ_properties[2, 0]),
-    )
-    perfuse = jnp.where(
-        medium_kinds == 0,
-        organ_properties[0, 1],
-        jnp.where(medium_kinds == 1, organ_properties[1, 1], organ_properties[2, 1]),
-    )
-    source = absorb * dose_sum
-    present_thermal = thermal_increase
-    for _ in range(HEAT_STEPS):
-        padded = padded_2(present_thermal, (("term", 1), ("pencil", 0)), 1)
-        center, near_sum = stencil_sum(padded)
-        present_thermal = heat_update(center, near_sum, perfuse, source)
-    return (final_brick, present_thermal)
+    )(pres, prior, loc, spec, jnp.asarray(z_table()), jnp.asarray(x_table()), kinds, thermal, props)
 
 
 def solution(mesh):
     return jax.shard_map(
-        on_device,
+        wave,
         mesh=mesh,
         in_specs=(
             P("pencil", None, None),

time: 206 us -> 185 us (0.90); the launches traced: 203 us -> 184 us
  Pallas kernels: 152 us -> 179 us
  starting transfers between devices: 26.3 us -> 0 us
  other arithmetic: 12 us -> 0 us
  waiting for transfers between devices: 7.51 us -> 0 us
    pallas_call x1, Pallas kernels: 152 us -> 179 us  [wave(): pl.pallas_call(wave_kernel, name='wave', out_shape=(brick, brick), in_spe...]
    ppermute x8 -> x0, starting transfers between devices: 26.3 us -> none  [the longest x4 13.9 us: padded_2(): lax.ppermute(lax.slice_in_dim(block, 0, width, axis=dim), axis, backward)]
    add x2 -> x0, other arithmetic: 11.2 us -> none  [heat_update(): center + DIFFUSION * (near_sum - 6.0 * center) - perfuse * center + source]
    ppermute x8 -> x0, waiting for transfers between devices: 7.51 us -> none  [the longest x4 7.5 us: padded_2(): lax.ppermute(lax.slice_in_dim(block, block.shape[dim] - width, None, axis...]
    unnamed x5 -> x3, local copies, waits for them, and re-layouts: 1.57 us -> 4.47 us
    slice x3 -> x0, local copies, waits for them, and re-layouts: 2.75 us -> none  [the longest x1 1.55 us: on_device(): organ_properties[0, 1]]
  transfers between devices with their start and end apart: 8 -> 0, of which waited for: 3 -> 0; matrix products, arithmetic and copies ran while one was open for 1% -> 0% of each run, Pallas kernels for 75% -> 0%
where the time goes in v2:
time: 185 us; the launch traced here: 184 us
  Pallas kernels  179 us (97%)
  local copies, waits for them, and re-layouts  4.47 us (2%)
    pallas_call x1, Pallas kernels, wave(): pl.pallas_call(wave_kernel, name='wave', out_shape=(brick, brick), in_spe...  179 us
    unnamed x3, local copies, waits for them, and re-layouts  4.47 us

profile of v2, /device:TPU:33, one launch (start us, length us, event | category | flops | bytes accessed | tf_op | source)
XLA Modules:
  0.0 184.4 jit_solution(3271265122853999305)
XLA Ops:
  0.6 1.3 copy.11.props
  2.0 179.3 %wave.1 = (f32[32,2,512]{2,1,0:T(2,128)}, f32[32,2,512]{2,1,0:T(2,128)}) custom-call(f32[32,16,512]{2,1,0:T(8,128)} %pres.1, f32[32,16,512]{2,1,0:T(8,128)} %prior.1, f32[2,32,16,512]{3,2,1,0:T(8,128)} %loc.1, f32[2,16,32,512]{3,2,1,0:T(8,128)} %spec.1, bf16[2,512,512]{2,1,0:T(8,128)(2,1)} %constant.4.clone.ztab, ...), custom_call_target="tpu_custom_call" | custom-call | tf_op jit(solution)/shard_map/wave/pallas_call | solution.py:634
  181.3 1.6 copy.14
  182.9 1.6 copy.15

commit v3 on v2

--- a/solution.py
+++ b/solution.py
@@ -24,6 +24,13 @@
 SCALE = 2.0 / (NX * NY * NZ)
 
 
+PENCIL_ORDER = (
+    (1, 0, 0), (0, 1, 0), (3, 1, 1), (2, 0, 0), (0, 1, 1), (1, 1, 0), (3, 0, 0), (2, 1, 1),
+    (1, 0, 1), (3, 1, 0), (2, 0, 1), (2, 1, 0), (3, 0, 1), (1, 1, 1), (0, 0, 1),
+)
+TERM_ORDER = ((1, 0), (0, 1), (3, 1), (2, 0), (3, 0), (1, 1), (2, 1))
+
+
 def high_low(table):
     high = table.astype(BF16)
     low = (table - high.astype(np.float32)).astype(BF16)
@@ -36,14 +43,14 @@
     for h in range(2):
         for p in range(NP):
             for i in range(8):
-                s = 8 * h + i
-                if s == 0 and p == 8:
+                if h == 1 and i == 0 and p == 8:
                     rows[h, p, 0, i] = 1.0
                     rows[h, p, 1, i] = 1.0 - 2.0 * (z % 2)
                     continue
-                kz = 32 * p + s
-                if s == 0 and p < 8:
-                    kz = 32 * p + 16
+                j = 8 * h + i
+                if i == 0:
+                    j = 8 if h == 0 else (16 if p < 8 else 0)
+                kz = 32 * p + j
                 angle = 2.0 * math.pi * ((kz * z) % NZ) / NZ
                 rows[h, p, 0, i] = np.cos(angle)
                 rows[h, p, 1, i] = -np.sin(angle)
@@ -134,7 +141,7 @@
     pres_v, prior_v, loc_v, lr, spec_v, srecv, row0, row0r, amp, bmp, zt, xt,
     kind_v, heat_v, absorb, perfuse, heat, field, hxs, hx, hy,
     cur, prev, dose, fsend, frecv, vsend, agb, w, xo, snd, rcv, psend, rsr,
-    lsem, ssem, sx, fs, fr, gs, gr, as0, ar0, as1, ar1, rs, rr, hs, hr,
+    lsem, sx, fs, fr, gs, gr, as0, ar0, as1, ar1, rs, rr, hs, hr,
 ):
     t = lax.axis_index("term")
     p = lax.axis_index("pencil")
@@ -152,46 +159,37 @@
     loads = [
         pltpu.make_async_copy(src, dst, lsem.at[i])
         for i, (src, dst) in enumerate(
-            [(pres, pres_v), (ztab, zt), (xtab, xt), (spec, spec_v), (prior, prior_v), (loc, loc_v), (kinds, kind_v), (thermal, heat_v)]
+            [
+                (pres, pres_v), (ztab, zt), (thermal, heat_v), (kinds, kind_v),
+                (spec, spec_v), (xtab, xt), (prior, prior_v), (loc, loc_v),
+            ]
         )
     ]
     for load in loads:
         load.start()
 
-    pl.semaphore_wait(barrier, NP + NT - 2)
-
     def remote(src, dst, send, recv, device):
         return pltpu.make_async_remote_copy(
             src_ref=src, dst_ref=dst, send_sem=send, recv_sem=recv, device_id=device, device_id_type=MESH
         )
 
+    def pencil_peers():
+        for dx, dy, dc in PENCIL_ORDER:
+            yield (
+                lax.rem(p // 4 + dx, 4) * 4 + lax.rem(lax.rem(p // 2, 2) + dy, 2) * 2 + lax.rem(lax.rem(p, 2) + dc, 2)
+            )
+
+    def term_peers():
+        for dz, dy in TERM_ORDER:
+            yield lax.rem(t // 2 + dz, 4) * 2 + lax.rem(lax.rem(t, 2) + dy, 2)
+
     mirror = (t, NP - 1 - p)
-    swap = remote(spec.at[:, :, pl.ds(16, 16), :], srecv, sx.at[0], sx.at[1], mirror)
-    swap.start()
-
-    loads[0].wait()
-    for y in range(2):
-        for x in range(XR):
-            row = y * XR + (x % 2) * 16 + x // 2
-            cur[pl.ds(row, 1), :] = pres_v[x, pl.ds(2 * t + y, 1), :]
-    loads[3].wait()
-    for q in range(2):
-        row0[pl.ds(16 * q, 16), 0, :] = spec_v[q, :, 0, :]
+    swaps = [
+        remote(spec.at[:, :, pl.ds(24 - 8 * h, 8), :], srecv.at[h], sx.at[h], sx.at[2 + h], mirror)
+        for h in range(2)
+    ]
     give = jnp.where(p == 0, 8, lax.rem(NP - p, NP))
-    rowcopy = remote(row0, row0r, sx.at[2], sx.at[3], (t, give))
-
-    @pl.when(p < 8)
-    def _():
-        rowcopy.start()
-
-    loads[4].wait()
-    for y in range(2):
-        for x in range(XR):
-            row = y * XR + (x % 2) * 16 + x // 2
-            prev[pl.ds(row, 1), :] = prior_v[x, pl.ds(2 * t + y, 1), :]
-    dose[...] = jnp.zeros_like(dose)
-    loads[1].wait()
-    loads[2].wait()
+    rowcopy = remote(row0, row0r, sx.at[4], sx.at[5], (t, give))
 
     lane = lax.broadcasted_iota(jnp.int32, (8, 128), 1)
     sub = lax.broadcasted_iota(jnp.int32, (8, 128), 0)
@@ -255,18 +253,22 @@
         return mine + DIFFUSION * (near - 6.0 * mine) - perfuse[rows, :] * mine
 
     def heat_begin():
-        loads[6].wait()
-        loads[7].wait()
+        loads[2].wait()
         for y in range(2):
             for x in range(XR):
                 row = y * XR + (x % 2) * 16 + x // 2
                 field[0, pl.ds(row, 1), :] = heat_v[x, pl.ds(y, 1), :]
+
+    def heat_coefficients():
+        loads[3].wait()
+        for y in range(2):
+            for x in range(XR):
+                row = y * XR + (x % 2) * 16 + x // 2
                 kind = kind_v[x, pl.ds(y, 1), :]
                 for ref, j in ((absorb, 0), (perfuse, 1)):
                     ref[pl.ds(row, 1), :] = jnp.where(
                         kind == 0, props[0, j], jnp.where(kind == 1, props[1, j], props[2, j])
                     )
-        halo_start(0)
 
     def heat_middle():
         halo_wait(0)
@@ -284,53 +286,56 @@
     def heat_finish():
         field[2] = absorb[...] * dose[...]
         halo_start(2)
+        for y in range(2):
+            for x in range(XR):
+                row = y * XR + (x % 2) * 16 + x // 2
+                final_o[x, pl.ds(y, 1), :] = cur[pl.ds(row, 1), :]
         halo_wait(2)
         for y in range(2):
             for c in range(2):
                 rows = pl.ds(32 * y + 16 * c, 16)
                 heat[rows, :] = heat[rows, :] + (field[2, rows, :] + heat_apply(2, y, c))
 
-    def build_amp():
-        swap.wait()
-
-        @pl.when(p < 8)
-        def _():
-            rowcopy.wait_send()
-
-        @pl.when(p >= 8)
-        def _():
-            rowcopy.wait_recv()
+    def build_amp(h):
+        swaps[h].wait()
+        if h == 1:
+
+            @pl.when(p < 8)
+            def _():
+                rowcopy.wait_send()
+
+            @pl.when(p >= 8)
+            def _():
+                rowcopy.wait_recv()
 
         low_p = jnp.where(p < 8, 1, 0)
+        special = pl.multiple_of(16 * low_p, 8)
 
         @pl.loop(0, 32)
         def _(n):
             q = n // 16
             ky = lax.rem(n, 16)
             kr = lax.rem(16 - ky, 16)
-            pick_own = (sub == 0) & (low_p == 1)
             pick_row = (sub == 0) & (low_p == 0)
-            mirrored = [[], []]
+            mirrored = []
             for a in range(4):
                 cols = pl.ds(128 * a, 128)
-                r0 = srecv[q, kr, pl.ds(0, 8), cols]
-                r1 = srecv[q, kr, pl.ds(8, 8), cols]
-                extra = jnp.broadcast_to(row0r[16 * q + kr, :, cols], (8, 128))
-                f0 = jnp.take_along_axis(r0, flip, axis=0)
-                f1 = jnp.take_along_axis(r1, flip, axis=0)
-                m0 = jnp.where(sub == 0, r0, f1)
-                m0 = jnp.where(pick_row, extra, m0)
-                m1 = jnp.where(sub == 0, r1, f0)
-                mirrored[0].append(m0)
-                mirrored[1].append(m1)
-            for h in range(2):
-                rev = reverse_lanes(mirrored[h])
-                for a in range(4):
-                    cols = pl.ds(128 * a, 128)
-                    own = spec_v[q, ky, pl.ds(8 * h, 8), cols]
-                    if h == 0:
-                        own = jnp.where(pick_own, spec_v[q, ky, pl.ds(16, 8), cols], own)
-                    amp[q, ky, pl.ds(8 * h, 8), cols] = own + rev[a]
+                m = jnp.take_along_axis(srecv[h, q, kr, :, cols], flip, axis=0)
+                if h == 1:
+                    extra = jnp.broadcast_to(row0r[16 * q + kr, :, cols], (8, 128))
+                    m = jnp.where(pick_row, extra, m)
+                mirrored.append(m)
+            mirrored = reverse_lanes(mirrored)
+            for a in range(4):
+                cols = pl.ds(128 * a, 128)
+                if h == 0:
+                    first, rest = spec_v[q, ky, pl.ds(8, 8), cols], spec_v[q, ky, pl.ds(0, 8), cols]
+                else:
+                    first, rest = spec_v[q, ky, pl.ds(special, 8), cols], spec_v[q, ky, pl.ds(8, 8), cols]
+                amp[q, ky, pl.ds(8 * h, 8), cols] = jnp.where(sub == 0, first, rest) + mirrored[a]
+
+        if h == 0:
+            return
 
         @pl.when(p == 8)
         def _():
@@ -350,8 +355,8 @@
                     cols = pl.ds(128 * a, 128)
                     last = spec_v[q, ky, pl.ds(0, 8), cols] + own_r[a]
                     first = jnp.broadcast_to(row0r[16 * q + ky, :, cols], (8, 128)) + zero_r[a]
-                    old = amp[q, ky, pl.ds(0, 8), cols]
-                    amp[q, ky, pl.ds(0, 8), cols] = jnp.where(sub == 0, 0.25 * (first + last), old)
+                    old = amp[q, ky, pl.ds(8, 8), cols]
+                    amp[q, ky, pl.ds(8, 8), cols] = jnp.where(sub == 0, 0.25 * (first + last), old)
                     bmp[q, ky, :, cols] = jnp.where(sub == 0, 0.25 * (first - last), 0.0)
 
     def y_stage(re, im, weight, store):
@@ -370,8 +375,7 @@
     def wait_bytes(ref, sem):
         pltpu.make_async_copy(ref, ref, sem).wait()
 
-    @pl.loop(0, WAVE_STEPS)
-    def _(step):
+    def forward_z():
         b = split(cur[...])
         b = tuple(jnp.concatenate([v, v], axis=0) for v in b)
         out = dot3((zt[0], zt[1]), b, 1, 1).reshape(2, NP, 2, 8, 128)
@@ -379,11 +383,36 @@
         for h in range(2):
             fsend[:, pl.ds(8 * h, 8), :] = jnp.where(wide < 64, out[h, :, 0], out[h, :, 1])
 
-        @pl.loop(1, NP)
-        def _(o):
-            d = lax.rem(p + o, NP)
+    def forward_send(step):
+        for d in pencil_peers():
             remote(fsend.at[d], frecv.at[step, p], fs.at[0], fr.at[step], (t, d)).start()
 
+    loads[0].wait()
+    for y in range(2):
+        for x in range(XR):
+            row = y * XR + (x % 2) * 16 + x // 2
+            cur[pl.ds(row, 1), :] = pres_v[x, pl.ds(2 * t + y, 1), :]
+    loads[1].wait()
+    forward_z()
+    heat_begin()
+    loads[4].wait()
+    for q in range(2):
+        row0[pl.ds(16 * q, 16), 0, :] = spec_v[q, :, 0, :]
+
+    pl.semaphore_wait(barrier, NP + NT - 2)
+    forward_send(0)
+    halo_start(0)
+
+    @pl.when(p < 8)
+    def _():
+        rowcopy.start()
+
+    for swap in swaps:
+        swap.start()
+    loads[5].wait()
+
+    @pl.loop(0, WAVE_STEPS)
+    def _(step):
         frecv[step, p] = fsend[p]
         wait_bytes(frecv.at[step, pl.ds(0, NP - 1)], fr.at[step])
 
@@ -410,20 +439,22 @@
 
         for h in range(2):
 
-            @pl.loop(1, NT)
-            def _(o):
-                d = lax.rem(t + o, NT)
+            for d in term_peers():
                 remote(vsend.at[h], agb.at[step, h, t], gs.at[h], gr.at[step, h], (d, p)).start()
 
             agb[step, h, t] = vsend[h]
 
         @pl.when(step == 0)
         def _():
-            heat_begin()
+            loads[6].wait()
+            for y in range(2):
+                for x in range(XR):
+                    row = y * XR + (x % 2) * 16 + x // 2
+                    prev[pl.ds(row, 1), :] = prior_v[x, pl.ds(2 * t + y, 1), :]
+            dose[...] = jnp.zeros_like(dose)
+            heat_coefficients()
             heat_middle()
-            heat_late()
-            build_amp()
-            loads[5].wait()
+            loads[7].wait()
             @pl.loop(0, 8)
             def _(n):
                 q = n // 4
@@ -440,6 +471,11 @@
                             lr[q, y, pl.ds(16 * c + 8 * i, 8), cols] = jnp.where(sub < 4, pair[0], pair[1])
 
         for h in range(2):
+
+            @pl.when(step == 0)
+            def _():
+                build_amp(h)
+
             wait_bytes(agb.at[step, h, pl.ds(0, NT - 1)], gr.at[step, h])
 
             @pl.loop(0, 4)
@@ -459,7 +495,7 @@
                     store,
                 )
 
-            if h == 0:
+            if h == 1:
 
                 @pl.when(p == 8)
                 def _():
@@ -471,8 +507,8 @@
                         index = (128 - lane) % 128
 
                         def load(y, ri):
-                            v0 = jnp.take_along_axis(agb[step, 0, y // 2, y % 2, ri, :, near], index, axis=1)
-                            v1 = jnp.take_along_axis(agb[step, 0, y // 2, y % 2, ri, :, far], index, axis=1)
+                            v0 = jnp.take_along_axis(agb[step, 1, y // 2, y % 2, ri, :, near], index, axis=1)
+                            v1 = jnp.take_along_axis(agb[step, 1, y // 2, y % 2, ri, :, far], index, axis=1)
                             return jnp.where(lane == 0, v0, v1)
 
                         def weight(q, ky):
@@ -506,43 +542,43 @@
                     cols = pl.ds(pl.multiple_of(ra * 128, 128), 128)
                     tiles = exchange_groups([xo[i % 2, 4 * yh + i // 2, :, cols] for i in range(8)])
                     for i in range(8):
-                        snd[h, first + i, yh, q, ri] = tiles[i]
-
-            if h == 0:
-
-                @pl.loop(1, NP)
-                def _(o):
-                    d = lax.rem(p + o, NP)
-                    remote(snd.at[0, d], rcv.at[step, 0, p], as0.at[0], ar0.at[step], (t, d)).start()
-
-            else:
+                        snd[h, first + i, q, yh, ri] = tiles[i]
+
+                if h == 0:
+                    for d in pencil_peers():
+                        remote(
+                            snd.at[0, d, q], rcv.at[step, 0, p, q], as0.at[0], ar0.at[step], (t, d)
+                        ).start()
+
+            if h == 1:
 
                 @pl.loop(0, 4)
                 def _(i):
                     yh = lax.rem(t // 2 + 1 + i, 4)
-
-                    @pl.loop(1, NP)
-                    def _(o):
-                        d = lax.rem(p + o, NP)
+                    for d in pencil_peers():
                         remote(
-                            snd.at[1, d, yh], rcv.at[step, 1, p, yh], as1.at[0], ar1.at[step, yh], (t, d)
+                            snd.at[1, d, :, yh], rcv.at[step, 1, p, :, yh], as1.at[0], ar1.at[step, yh], (t, d)
                         ).start()
 
             rcv[step, h, p] = snd[h, p]
 
         for h in range(2):
             wait_bytes(agb.at[step, h, pl.ds(0, NT - 1)], gs.at[h])
+
+        @pl.when(step == 1)
+        def _():
+            heat_late()
 
         wait_bytes(rcv.at[step, 0, pl.ds(0, NP - 1)], ar0.at[step])
 
         @pl.loop(0, 4)
         def _(i):
             yh = lax.rem(t // 2 + 1 + i, 4)
-            wait_bytes(rcv.at[step, 1, pl.ds(0, NP - 1), yh], ar1.at[step, yh])
+            wait_bytes(rcv.at[step, 1, pl.ds(0, NP - 1), :, yh], ar1.at[step, yh])
             total = None
             for q in range(2):
                 d = jnp.concatenate(
-                    [rcv[step, h, :, yh, q].reshape(256, 128) for h in range(2)], axis=0
+                    [rcv[step, h, :, q, yh].reshape(256, 128) for h in range(2)], axis=0
                 )
                 field = dot3(split(d), (zt[0], zt[1]), 0, 0)
                 field = field * lr[q, pl.ds(4 * yh, 4)].reshape(128, 512)
@@ -568,11 +604,15 @@
         prev[...] = cur[...]
         cur[...] = advanced
 
+        @pl.when(step == 0)
+        def _():
+            forward_z()
+            forward_send(1)
+
     heat_finish()
     for y in range(2):
         for x in range(XR):
             row = y * XR + (x % 2) * 16 + x // 2
-            final_o[x, pl.ds(y, 1), :] = cur[pl.ds(row, 1), :]
             heat_o[x, pl.ds(y, 1), :] = heat[pl.ds(row, 1), :]
 
 
@@ -586,7 +626,7 @@
         pltpu.VMEM((2, XR, NY, NZ), F32),
         pltpu.VMEM((2, NY, XR, NZ), F32),
         pltpu.VMEM((2, NY, 32, NX), F32),
-        pltpu.VMEM((2, NY, 16, NX), F32),
+        pltpu.VMEM((2, 2, NY, 8, NX), F32),
         pltpu.VMEM((32, 1, NX), F32),
         pltpu.VMEM((32, 1, NX), F32),
         pltpu.VMEM((2, NY, 16, NX), F32),
@@ -611,13 +651,12 @@
         pltpu.VMEM((2, 2, NT, 2, 2, 8, NX), F32),
         pltpu.VMEM((2, 2, NY, 8, NX), F32),
         pltpu.VMEM((2, NY, 8, NX), F32),
-        pltpu.VMEM((2, NP, 4, 2, 2, 8, 128), F32),
-        pltpu.VMEM((2, 2, NP, 4, 2, 2, 8, 128), F32),
+        pltpu.VMEM((2, NP, 2, 4, 2, 8, 128), F32),
+        pltpu.VMEM((2, 2, NP, 2, 4, 2, 8, 128), F32),
         pltpu.VMEM((NT, 64, NZ), F32),
         pltpu.VMEM((2, NT, 64, NZ), F32),
         pltpu.SemaphoreType.DMA((8,)),
-        pltpu.SemaphoreType.DMA((1,)),
-        pltpu.SemaphoreType.DMA((4,)),
+        pltpu.SemaphoreType.DMA((6,)),
         pltpu.SemaphoreType.DMA((1,)),
         pltpu.SemaphoreType.DMA((2,)),
         pltpu.SemaphoreType.DMA((2,)),

time: 185 us -> 160 us (0.86)
  Pallas kernels: 179 us -> 153 us
    pallas_call x1, Pallas kernels: 179 us -> 153 us  [wave(): pl.pallas_call(wave_kernel, name='wave', out_shape=(brick, brick), in_spe...]
where the time goes in v3:
time: 160 us; the launch traced here: 158 us
  Pallas kernels  153 us (96%)
  local copies, waits for them, and re-layouts  4.47 us (3%)
    pallas_call x1, Pallas kernels, wave(): pl.pallas_call(wave_kernel, name='wave', out_shape=(brick, brick), in_spe...  153 us
    unnamed x3, local copies, waits for them, and re-layouts  4.47 us

profile of v3, /device:TPU:33, one launch (start us, length us, event | category | flops | bytes accessed | tf_op | source)
XLA Modules:
  0.0 157.9 jit_solution(6295837112593739031)
XLA Ops:
  0.6 1.3 copy.11.props
  2.0 152.8 %wave.1 = (f32[32,2,512]{2,1,0:T(2,128)}, f32[32,2,512]{2,1,0:T(2,128)}) custom-call(f32[32,16,512]{2,1,0:T(8,128)} %pres.1, f32[32,16,512]{2,1,0:T(8,128)} %prior.1, f32[2,32,16,512]{3,2,1,0:T(8,128)} %loc.1, f32[2,16,32,512]{3,2,1,0:T(8,128)} %spec.1, bf16[2,512,512]{2,1,0:T(8,128)(2,1)} %constant.4.clone.ztab, ...), custom_call_target="tpu_custom_call" | custom-call | tf_op jit(solution)/shard_map/wave/pallas_call | solution.py:673
  154.8 1.6 copy.14
  156.3 1.6 copy.15

commit v4 on v3

--- a/solution.py
+++ b/solution.py
@@ -28,7 +28,9 @@
     (1, 0, 0), (0, 1, 0), (3, 1, 1), (2, 0, 0), (0, 1, 1), (1, 1, 0), (3, 0, 0), (2, 1, 1),
     (1, 0, 1), (3, 1, 0), (2, 0, 1), (2, 1, 0), (3, 0, 1), (1, 1, 1), (0, 0, 1),
 )
-TERM_ORDER = ((1, 0), (0, 1), (3, 1), (2, 0), (3, 0), (1, 1), (2, 1))
+
+
+TERM_ORDER = ((2, 0), (0, 1), (1, 1), (3, 1), (1, 0), (3, 0), (2, 1))
 
 
 def high_low(table):
@@ -140,8 +142,8 @@
     pres, prior, loc, spec, ztab, xtab, kinds, thermal, props, final_o, heat_o,
     pres_v, prior_v, loc_v, lr, spec_v, srecv, row0, row0r, amp, bmp, zt, xt,
     kind_v, heat_v, absorb, perfuse, heat, field, hxs, hx, hy,
-    cur, prev, dose, fsend, frecv, vsend, agb, w, xo, snd, rcv, psend, rsr,
-    lsem, sx, fs, fr, gs, gr, as0, ar0, as1, ar1, rs, rr, hs, hr,
+    cur, prev, dose, fsend, frecv, vsend, agb, w, xo, snd, rcv, psend, rsr, psum, ptake,
+    lsem, sx, fs, fr, gs, gr, gy, sent, came, rs, rr, ps, pr, hs, hr,
 ):
     t = lax.axis_index("term")
     p = lax.axis_index("pencil")
@@ -179,9 +181,15 @@
                 lax.rem(p // 4 + dx, 4) * 4 + lax.rem(lax.rem(p // 2, 2) + dy, 2) * 2 + lax.rem(lax.rem(p, 2) + dc, 2)
             )
 
-    def term_peers():
-        for dz, dy in TERM_ORDER:
-            yield lax.rem(t // 2 + dz, 4) * 2 + lax.rem(lax.rem(t, 2) + dy, 2)
+    z_place, y_place = t // 2, lax.rem(t, 2)
+    partner = t + 1 - 2 * y_place
+
+    def chunk(i):
+        return lax.rem(z_place + lax.rem(2 + 3 * i + 3 * (i // 2) + 2 * (i // 3), 4), 4)
+
+    def z_peers():
+        for dz in (1, 3, 2):
+            yield lax.rem(z_place + dz, 4) * 2 + y_place
 
     mirror = (t, NP - 1 - p)
     swaps = [
@@ -311,28 +319,31 @@
         low_p = jnp.where(p < 8, 1, 0)
         special = pl.multiple_of(16 * low_p, 8)
 
-        @pl.loop(0, 32)
-        def _(n):
-            q = n // 16
-            ky = lax.rem(n, 16)
-            kr = lax.rem(16 - ky, 16)
-            pick_row = (sub == 0) & (low_p == 0)
-            mirrored = []
-            for a in range(4):
-                cols = pl.ds(128 * a, 128)
-                m = jnp.take_along_axis(srecv[h, q, kr, :, cols], flip, axis=0)
-                if h == 1:
-                    extra = jnp.broadcast_to(row0r[16 * q + kr, :, cols], (8, 128))
-                    m = jnp.where(pick_row, extra, m)
-                mirrored.append(m)
-            mirrored = reverse_lanes(mirrored)
-            for a in range(4):
-                cols = pl.ds(128 * a, 128)
-                if h == 0:
-                    first, rest = spec_v[q, ky, pl.ds(8, 8), cols], spec_v[q, ky, pl.ds(0, 8), cols]
-                else:
-                    first, rest = spec_v[q, ky, pl.ds(special, 8), cols], spec_v[q, ky, pl.ds(8, 8), cols]
-                amp[q, ky, pl.ds(8 * h, 8), cols] = jnp.where(sub == 0, first, rest) + mirrored[a]
+        pick_row = (sub == 0) & (low_p == 0)
+
+        @pl.loop(0, 8)
+        def _(m4):
+            for j in range(4):
+                n = 4 * m4 + j
+                q = n // 16
+                ky = lax.rem(n, 16)
+                kr = lax.rem(16 - ky, 16)
+                mirrored = []
+                for a in range(4):
+                    cols = pl.ds(128 * a, 128)
+                    m = jnp.take_along_axis(srecv[h, q, kr, :, cols], flip, axis=0)
+                    if h == 1:
+                        extra = jnp.broadcast_to(row0r[16 * q + kr, :, cols], (8, 128))
+                        m = jnp.where(pick_row, extra, m)
+                    mirrored.append(m)
+                mirrored = reverse_lanes(mirrored)
+                for a in range(4):
+                    cols = pl.ds(128 * a, 128)
+                    if h == 0:
+                        first, rest = spec_v[q, ky, pl.ds(8, 8), cols], spec_v[q, ky, pl.ds(0, 8), cols]
+                    else:
+                        first, rest = spec_v[q, ky, pl.ds(special, 8), cols], spec_v[q, ky, pl.ds(8, 8), cols]
+                    amp[q, ky, pl.ds(8 * h, 8), cols] = jnp.where(sub == 0, first, rest) + mirrored[a]
 
         if h == 0:
             return
@@ -437,11 +448,13 @@
                         ]
         wait_bytes(fsend.at[pl.ds(0, NP - 1)], fs.at[0])
 
+        for dz, dy in TERM_ORDER:
+            d = lax.rem(z_place + dz, 4) * 2 + lax.rem(y_place + dy, 2)
+            remote(vsend.at[0], agb.at[step, 0, t], gs.at[0], gr.at[step, 0], (d, p)).start()
+        remote(vsend.at[1], agb.at[step, 1, t], gs.at[1], gy.at[step], (partner, p)).start()
+        for d in z_peers():
+            remote(vsend.at[1], agb.at[step, 1, t], gs.at[1], gr.at[step, 1], (d, p)).start()
         for h in range(2):
-
-            for d in term_peers():
-                remote(vsend.at[h], agb.at[step, h, t], gs.at[h], gr.at[step, h], (d, p)).start()
-
             agb[step, h, t] = vsend[h]
 
         @pl.when(step == 0)
@@ -476,7 +489,12 @@
             def _():
                 build_amp(h)
 
-            wait_bytes(agb.at[step, h, pl.ds(0, NT - 1)], gr.at[step, h])
+            wait_bytes(agb.at[step, h, pl.ds(0, NT - 1 - h)], gr.at[step, h])
+            if h == 0:
+                theirs = agb.at[step, 1, partner]
+                wait_bytes(theirs, gy.at[step])
+                for d in z_peers():
+                    remote(theirs, theirs, gs.at[1], gr.at[step, 1], (d, p)).start()
 
             @pl.loop(0, 4)
             def _(a):
@@ -533,34 +551,31 @@
                     lhs = split(jnp.concatenate(mix, axis=1))
                     xo[c] = dot3(lhs, (xt[c, 0], xt[c, 1]), 1, 0).reshape(16, 8, 512)
 
-                @pl.loop(0, 16)
-                def _(n):
-                    yh = n // 4
-                    ra = lax.rem(n, 4)
+                @pl.loop(0, 4)
+                def _(ra):
                     ri = ra // 2
                     first = 8 * lax.rem(ra, 2)
                     cols = pl.ds(pl.multiple_of(ra * 128, 128), 128)
-                    tiles = exchange_groups([xo[i % 2, 4 * yh + i // 2, :, cols] for i in range(8)])
-                    for i in range(8):
-                        snd[h, first + i, q, yh, ri] = tiles[i]
-
-                if h == 0:
-                    for d in pencil_peers():
-                        remote(
-                            snd.at[0, d, q], rcv.at[step, 0, p, q], as0.at[0], ar0.at[step], (t, d)
-                        ).start()
-
-            if h == 1:
-
-                @pl.loop(0, 4)
-                def _(i):
-                    yh = lax.rem(t // 2 + 1 + i, 4)
-                    for d in pencil_peers():
-                        remote(
-                            snd.at[1, d, :, yh], rcv.at[step, 1, p, :, yh], as1.at[0], ar1.at[step, yh], (t, d)
-                        ).start()
-
-            rcv[step, h, p] = snd[h, p]
+                    for yh in range(4):
+                        tiles = exchange_groups([xo[i % 2, 4 * yh + i // 2, :, cols] for i in range(8)])
+                        for i in range(8):
+                            snd[first + i, yh, h, q, ri] = tiles[i]
+
+            rcv[step, p, :, h] = snd[p, :, h]
+
+            @pl.loop(0, 2)
+            def _(i):
+                yh = chunk(i)
+                for d in pencil_peers():
+                    remote(
+                        snd.at[d, yh, h], rcv.at[step, p, yh, h], sent.at[0], came.at[step, yh], (t, d)
+                    ).start()
+
+        @pl.loop(2, 4)
+        def _(i):
+            yh = chunk(i)
+            for d in pencil_peers():
+                remote(snd.at[d, yh], rcv.at[step, p, yh], sent.at[0], came.at[step, yh], (t, d)).start()
 
         for h in range(2):
             wait_bytes(agb.at[step, h, pl.ds(0, NT - 1)], gs.at[h])
@@ -569,36 +584,43 @@
         def _():
             heat_late()
 
-        wait_bytes(rcv.at[step, 0, pl.ds(0, NP - 1)], ar0.at[step])
-
         @pl.loop(0, 4)
         def _(i):
-            yh = lax.rem(t // 2 + 1 + i, 4)
-            wait_bytes(rcv.at[step, 1, pl.ds(0, NP - 1), :, yh], ar1.at[step, yh])
+            yh = chunk(i)
+            wait_bytes(rcv.at[step, pl.ds(0, NP - 1), yh], came.at[step, yh])
             total = None
             for q in range(2):
                 d = jnp.concatenate(
-                    [rcv[step, h, :, q, yh].reshape(256, 128) for h in range(2)], axis=0
+                    [rcv[step, :, yh, h, q].reshape(256, 128) for h in range(2)], axis=0
                 )
                 field = dot3(split(d), (zt[0], zt[1]), 0, 0)
                 field = field * lr[q, pl.ds(4 * yh, 4)].reshape(128, 512)
                 total = field if total is None else total + field
-            psend[pl.ds(2 * yh, 2)] = total.reshape(2, 64, 512)
-            for j in range(2):
-                d = 2 * yh + j
-
-                @pl.when(d != t)
-                def _():
-                    remote(psend.at[d], rsr.at[step, t], rs.at[0], rr.at[step], (d, p)).start()
-
-        wait_bytes(snd.at[0, pl.ds(0, NP - 1)], as0.at[0])
-        wait_bytes(snd.at[1, pl.ds(0, NP - 1)], as1.at[0])
-        rsr[step, t] = psend[t]
-        wait_bytes(rsr.at[step, pl.ds(0, NT - 1)], rr.at[step])
-        wait_bytes(psend.at[pl.ds(0, NT - 1)], rs.at[0])
-        total = rsr[step, 0]
-        for i in range(1, NT):
-            total = total + rsr[step, i]
+            psend[yh] = total.reshape(2, 64, 512)
+
+            @pl.when(yh != z_place)
+            def _():
+                remote(
+                    psend.at[yh], rsr.at[step, z_place], rs.at[0], rr.at[step], (2 * yh + y_place, p)
+                ).start()
+
+        wait_bytes(snd.at[pl.ds(0, NP - 1)], sent.at[0])
+        wait_bytes(rsr.at[step, pl.ds(0, 3)], rr.at[step])
+
+        def z_sum(j):
+            total = psend[z_place, j]
+            for dz in range(1, 4):
+                total = total + rsr[step, lax.rem(z_place + dz, 4), j]
+            return total
+
+        psum[...] = z_sum(1 - y_place)
+        give_sum = remote(psum, ptake.at[step], ps.at[0], pr.at[step], (partner, p))
+        give_sum.start()
+        total = z_sum(y_place)
+        wait_bytes(psend.at[pl.ds(0, 3)], rs.at[0])
+        give_sum.wait_send()
+        wait_bytes(ptake.at[step], pr.at[step])
+        total = total + ptake[step]
         advanced = SCALE * total - prev[...]
         dose[...] = dose[...] + advanced * advanced
         prev[...] = cur[...]
@@ -651,20 +673,23 @@
         pltpu.VMEM((2, 2, NT, 2, 2, 8, NX), F32),
         pltpu.VMEM((2, 2, NY, 8, NX), F32),
         pltpu.VMEM((2, NY, 8, NX), F32),
-        pltpu.VMEM((2, NP, 2, 4, 2, 8, 128), F32),
-        pltpu.VMEM((2, 2, NP, 2, 4, 2, 8, 128), F32),
-        pltpu.VMEM((NT, 64, NZ), F32),
-        pltpu.VMEM((2, NT, 64, NZ), F32),
+        pltpu.VMEM((NP, 4, 2, 2, 2, 8, 128), F32),
+        pltpu.VMEM((2, NP, 4, 2, 2, 2, 8, 128), F32),
+        pltpu.VMEM((4, 2, 64, NZ), F32),
+        pltpu.VMEM((2, 4, 2, 64, NZ), F32),
+        pltpu.VMEM((64, NZ), F32),
+        pltpu.VMEM((2, 64, NZ), F32),
         pltpu.SemaphoreType.DMA((8,)),
         pltpu.SemaphoreType.DMA((6,)),
         pltpu.SemaphoreType.DMA((1,)),
         pltpu.SemaphoreType.DMA((2,)),
         pltpu.SemaphoreType.DMA((2,)),
         pltpu.SemaphoreType.DMA((2, 2)),
-        pltpu.SemaphoreType.DMA((1,)),
         pltpu.SemaphoreType.DMA((2,)),
         pltpu.SemaphoreType.DMA((1,)),
         pltpu.SemaphoreType.DMA((2, 4)),
+        pltpu.SemaphoreType.DMA((1,)),
+        pltpu.SemaphoreType.DMA((2,)),
         pltpu.SemaphoreType.DMA((1,)),
         pltpu.SemaphoreType.DMA((2,)),
         pltpu.SemaphoreType.DMA((3, 4)),

time: 160 us -> 147 us (0.919); the launches traced: 158 us -> 147 us
  Pallas kernels: 153 us -> 142 us
    pallas_call x1, Pallas kernels: 153 us -> 142 us  [wave(): pl.pallas_call(wave_kernel, name='wave', out_shape=(brick, brick), in_spe...]
where the time goes in v4:
time: 147 us
  Pallas kernels  142 us (97%)
  local copies, waits for them, and re-layouts  4.47 us (3%)
    pallas_call x1, Pallas kernels, wave(): pl.pallas_call(wave_kernel, name='wave', out_shape=(brick, brick), in_spe...  142 us
    unnamed x3, local copies, waits for them, and re-layouts  4.47 us

profile of v4, /device:TPU:33, one launch (start us, length us, event | category | flops | bytes accessed | tf_op | source)
XLA Modules:
  0.0 146.7 jit_solution(9730591085591374823)
XLA Ops:
  0.6 1.3 copy.11.props
  2.0 141.6 %wave.1 = (f32[32,2,512]{2,1,0:T(2,128)}, f32[32,2,512]{2,1,0:T(2,128)}) custom-call(f32[32,16,512]{2,1,0:T(8,128)} %pres.1, f32[32,16,512]{2,1,0:T(8,128)} %prior.1, f32[2,32,16,512]{3,2,1,0:T(8,128)} %loc.1, f32[2,16,32,512]{3,2,1,0:T(8,128)} %spec.1, bf16[2,512,512]{2,1,0:T(8,128)(2,1)} %constant.4.clone.ztab, ...), custom_call_target="tpu_custom_call" | custom-call | tf_op jit(solution)/shard_map/wave/pallas_call | solution.py:698
  143.6 1.6 %copy.14 = f32[32,2,512]{2,1,0:T(2,128)} copy(f32[32,2,512]{2,1,0:T(2,128)} %get-tuple-element.4) | data formatting | bytes 262144
  145.2 1.6 %copy.15 = f32[32,2,512]{2,1,0:T(2,128)} copy(f32[32,2,512]{2,1,0:T(2,128)} %get-tuple-element.5) | data formatting | bytes 262144

commit v5 on v4

--- a/solution.py
+++ b/solution.py
@@ -139,7 +139,7 @@
 
 
 def wave_kernel(
-    pres, prior, loc, spec, ztab, xtab, kinds, thermal, props, final_o, heat_o,
+    pres, prior, loc, spec, ztab, xtab, kinds, thermal, props, result,
     pres_v, prior_v, loc_v, lr, spec_v, srecv, row0, row0r, amp, bmp, zt, xt,
     kind_v, heat_v, absorb, perfuse, heat, field, hxs, hx, hy,
     cur, prev, dose, fsend, frecv, vsend, agb, w, xo, snd, rcv, psend, rsr, psum, ptake,
@@ -275,7 +275,7 @@
                 kind = kind_v[x, pl.ds(y, 1), :]
                 for ref, j in ((absorb, 0), (perfuse, 1)):
                     ref[pl.ds(row, 1), :] = jnp.where(
-                        kind == 0, props[0, j], jnp.where(kind == 1, props[1, j], props[2, j])
+                        kind == 0, props[j, 0], jnp.where(kind == 1, props[j, 1], props[j, 2])
                     )
 
     def heat_middle():
@@ -297,7 +297,7 @@
         for y in range(2):
             for x in range(XR):
                 row = y * XR + (x % 2) * 16 + x // 2
-                final_o[x, pl.ds(y, 1), :] = cur[pl.ds(row, 1), :]
+                result[0, x, pl.ds(y, 1), :] = cur[pl.ds(row, 1), :]
         halo_wait(2)
         for y in range(2):
             for c in range(2):
@@ -412,14 +412,7 @@
 
     pl.semaphore_wait(barrier, NP + NT - 2)
     forward_send(0)
-    halo_start(0)
-
-    @pl.when(p < 8)
-    def _():
-        rowcopy.start()
-
-    for swap in swaps:
-        swap.start()
+    swaps[0].start()
     loads[5].wait()
 
     @pl.loop(0, WAVE_STEPS)
@@ -459,6 +452,13 @@
 
         @pl.when(step == 0)
         def _():
+            swaps[1].start()
+
+            @pl.when(p < 8)
+            def _():
+                rowcopy.start()
+
+            halo_start(0)
             loads[6].wait()
             for y in range(2):
                 for x in range(XR):
@@ -466,7 +466,6 @@
                     prev[pl.ds(row, 1), :] = prior_v[x, pl.ds(2 * t + y, 1), :]
             dose[...] = jnp.zeros_like(dose)
             heat_coefficients()
-            heat_middle()
             loads[7].wait()
             @pl.loop(0, 8)
             def _(n):
@@ -580,6 +579,10 @@
         for h in range(2):
             wait_bytes(agb.at[step, h, pl.ds(0, NT - 1)], gs.at[h])
 
+        @pl.when(step == 0)
+        def _():
+            heat_middle()
+
         @pl.when(step == 1)
         def _():
             heat_late()
@@ -635,11 +638,11 @@
     for y in range(2):
         for x in range(XR):
             row = y * XR + (x % 2) * 16 + x // 2
-            heat_o[x, pl.ds(y, 1), :] = heat[pl.ds(row, 1), :]
+            result[1, x, pl.ds(y, 1), :] = heat[pl.ds(row, 1), :]
 
 
 def wave(pres, prior, loc, spec, kinds, props, thermal):
-    brick = jax.ShapeDtypeStruct((XR, 2, NZ), F32)
+    bricks = jax.ShapeDtypeStruct((2, XR, 2, NZ), F32)
     any_spec = pl.BlockSpec(memory_space=pl.ANY)
     vmem_spec = pl.BlockSpec(memory_space=pltpu.VMEM)
     scratch = [
@@ -695,17 +698,18 @@
         pltpu.SemaphoreType.DMA((3, 4)),
         pltpu.SemaphoreType.DMA((3, 4)),
     ]
-    return pl.pallas_call(
+    both = pl.pallas_call(
         wave_kernel,
         name="wave",
-        out_shape=(brick, brick),
+        out_shape=bricks,
         in_specs=[any_spec] * 8 + [pl.BlockSpec(memory_space=pltpu.SMEM)],
-        out_specs=(vmem_spec, vmem_spec),
+        out_specs=vmem_spec,
         scratch_shapes=scratch,
         compiler_params=pltpu.CompilerParams(
             collective_id=0, has_side_effects=True, vmem_limit_bytes=60 * 2**20
         ),
-    )(pres, prior, loc, spec, jnp.asarray(z_table()), jnp.asarray(x_table()), kinds, thermal, props)
+    )(pres, prior, loc, spec, jnp.asarray(z_table()), jnp.asarray(x_table()), kinds, thermal, props.T)
+    return both[0], both[1]
 
 
 def solution(mesh):

time: 147 us -> 144 us (0.980); the launches traced: 147 us -> 142 us
  local copies, waits for them, and re-layouts: 4.47 us -> 1.69 us
  Pallas kernels: 142 us -> 140 us
    unnamed x3 -> x0, local copies, waits for them, and re-layouts: 4.47 us -> none
    pallas_call x1, Pallas kernels: 142 us -> 140 us  [wave(): pl.pallas_call(wave_kernel, name='wave', out_shape=bricks, in_specs=[any_...]
    squeeze x0 -> x1, local copies, waits for them, and re-layouts: none -> 1.69 us  [wave(): return (both[0], both[1])]
where the time goes in v5:
time: 144 us; the launch traced here: 142 us
  Pallas kernels  140 us (97%)
  local copies, waits for them, and re-layouts  1.69 us (1%)
    pallas_call x1, Pallas kernels, wave(): pl.pallas_call(wave_kernel, name='wave', out_shape=bricks, in_specs=[any_...  140 us

profile of v5, /device:TPU:33, one launch (start us, length us, event | category | flops | bytes accessed | tf_op | source)
XLA Modules:
  0.0 142.1 jit_solution(14626858526227044230)
XLA Ops:
  0.6 139.7 %wave.1 = f32[2,32,2,512]{3,2,1,0:T(2,128)} custom-call(f32[32,16,512]{2,1,0:T(8,128)} %pres.1, f32[32,16,512]{2,1,0:T(8,128)} %prior.1, f32[2,32,16,512]{3,2,1,0:T(8,128)} %loc.1, f32[2,16,32,512]{3,2,1,0:T(8,128)} %spec.1, bf16[2,512,512]{2,1,0:T(8,128)(2,1)} %constant.4.clone.ztab, bf16[2,2,512,512]{3,2,1,0:T(8,128)(2,1)} %constant.5.clone.xtab, ...), custom_call_target="tpu_custom_call" | custom-call | tf_op jit(solution)/shard_map/wave/pallas_call | solution.py:701
  140.4 1.7 %slice_bitcast_fusion = (f32[32,2,512]{2,1,0:T(2,128)}, f32[32,2,512]{2,1,0:T(2,128)}) fusion(f32[2,32,2,512]{3,2,1,0:T(2,128)} %wave.1), kind=kLoop, calls=%fused_computation | loop fusion | bytes 524288 | tf_op jit(solution)/shard_map/squeeze | solution.py:712

commit v6 on v5

--- a/solution.py
+++ b/solution.py
@@ -489,11 +489,6 @@
                 build_amp(h)
 
             wait_bytes(agb.at[step, h, pl.ds(0, NT - 1 - h)], gr.at[step, h])
-            if h == 0:
-                theirs = agb.at[step, 1, partner]
-                wait_bytes(theirs, gy.at[step])
-                for d in z_peers():
-                    remote(theirs, theirs, gs.at[1], gr.at[step, 1], (d, p)).start()
 
             @pl.loop(0, 4)
             def _(a):
@@ -541,24 +536,30 @@
                             store,
                         )
 
-            @pl.loop(0, 2)
-            def _(q):
-                low = [w[q, ri, :, :, pl.ds(0, 256)].reshape(128, 256) for ri in range(2)]
-                high = [w[q, ri, :, :, pl.ds(256, 256)].reshape(128, 256) for ri in range(2)]
-                for c in range(2):
-                    mix = [(lo + hi) if c == 0 else (lo - hi) for lo, hi in zip(low, high)]
-                    lhs = split(jnp.concatenate(mix, axis=1))
-                    xo[c] = dot3(lhs, (xt[c, 0], xt[c, 1]), 1, 0).reshape(16, 8, 512)
-
-                @pl.loop(0, 4)
-                def _(ra):
-                    ri = ra // 2
-                    first = 8 * lax.rem(ra, 2)
-                    cols = pl.ds(pl.multiple_of(ra * 128, 128), 128)
-                    for yh in range(4):
-                        tiles = exchange_groups([xo[i % 2, 4 * yh + i // 2, :, cols] for i in range(8)])
-                        for i in range(8):
-                            snd[first + i, yh, h, q, ri] = tiles[i]
+            if h == 0:
+                theirs = agb.at[step, 1, partner]
+                wait_bytes(theirs, gy.at[step])
+                for d in z_peers():
+                    remote(theirs, theirs, gs.at[1], gr.at[step, 1], (d, p)).start()
+
+            low = [w[:, ri, :, :, pl.ds(0, 256)].reshape(256, 256) for ri in range(2)]
+            high = [w[:, ri, :, :, pl.ds(256, 256)].reshape(256, 256) for ri in range(2)]
+            for c in range(2):
+                mix = [(lo + hi) if c == 0 else (lo - hi) for lo, hi in zip(low, high)]
+                lhs = split(jnp.concatenate(mix, axis=1))
+                xo[c] = dot3(lhs, (xt[c, 0], xt[c, 1]), 1, 0).reshape(2, 16, 8, 512)
+
+            @pl.loop(0, 8)
+            def _(n):
+                q = n // 4
+                ra = lax.rem(n, 4)
+                ri = ra // 2
+                first = 8 * lax.rem(ra, 2)
+                cols = pl.ds(pl.multiple_of(ra * 128, 128), 128)
+                for yh in range(4):
+                    tiles = exchange_groups([xo[i % 2, q, 4 * yh + i // 2, :, cols] for i in range(8)])
+                    for i in range(8):
+                        snd[first + i, yh, h, q, ri] = tiles[i]
 
             rcv[step, p, :, h] = snd[p, :, h]
 
@@ -591,14 +592,16 @@
         def _(i):
             yh = chunk(i)
             wait_bytes(rcv.at[step, pl.ds(0, NP - 1), yh], came.at[step, yh])
-            total = None
-            for q in range(2):
-                d = jnp.concatenate(
-                    [rcv[step, :, yh, h, q].reshape(256, 128) for h in range(2)], axis=0
-                )
-                field = dot3(split(d), (zt[0], zt[1]), 0, 0)
-                field = field * lr[q, pl.ds(4 * yh, 4)].reshape(128, 512)
-                total = field if total is None else total + field
+            d = jnp.concatenate(
+                [
+                    jnp.concatenate([rcv[step, :, yh, h, q].reshape(256, 128) for q in range(2)], axis=1)
+                    for h in range(2)
+                ],
+                axis=0,
+            )
+            fields = dot3(split(d), (zt[0], zt[1]), 0, 0)
+            total = fields[:128] * lr[0, pl.ds(4 * yh, 4)].reshape(128, 512)
+            total = total + fields[128:] * lr[1, pl.ds(4 * yh, 4)].reshape(128, 512)
             psend[yh] = total.reshape(2, 64, 512)
 
             @pl.when(yh != z_place)
@@ -675,7 +678,7 @@
         pltpu.VMEM((2, 2, 2, 8, NX), F32),
         pltpu.VMEM((2, 2, NT, 2, 2, 8, NX), F32),
         pltpu.VMEM((2, 2, NY, 8, NX), F32),
-        pltpu.VMEM((2, NY, 8, NX), F32),
+        pltpu.VMEM((2, 2, NY, 8, NX), F32),
         pltpu.VMEM((NP, 4, 2, 2, 2, 8, 128), F32),
         pltpu.VMEM((2, NP, 4, 2, 2, 2, 8, 128), F32),
         pltpu.VMEM((4, 2, 64, NZ), F32),

time: 144 us -> 144 us (level); the launches traced: 142 us -> 144 us
    pallas_call x1, Pallas kernels: 140 us -> 141 us  [wave(): pl.pallas_call(wave_kernel, name='wave', out_shape=bricks, in_specs=[any_...]
where the time goes in v6:
time: 144 us
  Pallas kernels  141 us (98%)
  local copies, waits for them, and re-layouts  1.69 us (1%)
    pallas_call x1, Pallas kernels, wave(): pl.pallas_call(wave_kernel, name='wave', out_shape=bricks, in_specs=[any_...  141 us

profile of v6, /device:TPU:33, one launch (start us, length us, event | category | flops | bytes accessed | tf_op | source)
XLA Modules:
  0.0 143.8 jit_solution(3028894890181613797)
XLA Ops:
  0.6 141.5 %wave.1 = f32[2,32,2,512]{3,2,1,0:T(2,128)} custom-call(f32[32,16,512]{2,1,0:T(8,128)} %pres.1, f32[32,16,512]{2,1,0:T(8,128)} %prior.1, f32[2,32,16,512]{3,2,1,0:T(8,128)} %loc.1, f32[2,16,32,512]{3,2,1,0:T(8,128)} %spec.1, bf16[2,512,512]{2,1,0:T(8,128)(2,1)} %constant.4.clone.ztab, bf16[2,2,512,512]{3,2,1,0:T(8,128)(2,1)} %constant.5.clone.xtab, ...), custom_call_target="tpu_custom_call" | custom-call | tf_op jit(solution)/shard_map/wave/pallas_call | solution.py:704
  142.1 1.7 %slice_bitcast_fusion = (f32[32,2,512]{2,1,0:T(2,128)}, f32[32,2,512]{2,1,0:T(2,128)}) fusion(f32[2,32,2,512]{3,2,1,0:T(2,128)} %wave.1), kind=kLoop, calls=%fused_computation | loop fusion | bytes 524288 | tf_op jit(solution)/shard_map/squeeze | solution.py:715

commit v7 on v6

--- a/solution.py
+++ b/solution.py
@@ -563,7 +563,7 @@
 
             rcv[step, p, :, h] = snd[p, :, h]
 
-            @pl.loop(0, 2)
+            @pl.loop(0, 3)
             def _(i):
                 yh = chunk(i)
                 for d in pencil_peers():
@@ -571,7 +571,7 @@
                         snd.at[d, yh, h], rcv.at[step, p, yh, h], sent.at[0], came.at[step, yh], (t, d)
                     ).start()
 
-        @pl.loop(2, 4)
+        @pl.loop(3, 4)
         def _(i):
             yh = chunk(i)
             for d in pencil_peers():

time: 144 us -> 145 us (level)
  Pallas kernels: 141 us -> 143 us
where the time goes in v7:
time: 145 us
  Pallas kernels  143 us (99%)
  local copies, waits for them, and re-layouts  1.69 us (1%)
    pallas_call x1, Pallas kernels, wave(): pl.pallas_call(wave_kernel, name='wave', out_shape=bricks, in_specs=[any_...  143 us

profile of v7, /device:TPU:33, one launch (start us, length us, event | category | flops | bytes accessed | tf_op | source)
XLA Modules:
  0.0 145.0 jit_solution(11496956404555297237)
XLA Ops:
  0.6 142.6 %wave.1 = f32[2,32,2,512]{3,2,1,0:T(2,128)} custom-call(f32[32,16,512]{2,1,0:T(8,128)} %pres.1, f32[32,16,512]{2,1,0:T(8,128)} %prior.1, f32[2,32,16,512]{3,2,1,0:T(8,128)} %loc.1, f32[2,16,32,512]{3,2,1,0:T(8,128)} %spec.1, bf16[2,512,512]{2,1,0:T(8,128)(2,1)} %constant.4.clone.ztab, bf16[2,2,512,512]{3,2,1,0:T(8,128)(2,1)} %constant.5.clone.xtab, ...), custom_call_target="tpu_custom_call" | custom-call | tf_op jit(solution)/shard_map/wave/pallas_call | solution.py:704
  143.3 1.7 %slice_bitcast_fusion = (f32[32,2,512]{2,1,0:T(2,128)}, f32[32,2,512]{2,1,0:T(2,128)}) fusion(f32[2,32,2,512]{3,2,1,0:T(2,128)} %wave.1), kind=kLoop, calls=%fused_computation | loop fusion | bytes 524288 | tf_op jit(solution)/shard_map/squeeze | solution.py:715
